TPU v7x, 512 devices: a whole 4x8x8 slice. The times are simulated.
512 devices in a mesh: gx: 16 (over y_hi, x, core), gy: 4 (over y_lo), gz: 8 (over z).
Axes of the slice: x: 4, y: 8 (y_hi: 2, y_lo: 4; y = y_hi * 4 + y_lo), z: 8, core: 2. Of those that a mesh axis runs over, the one named last changes fastest.
Arguments:
- velocity: float32 [3, 32, 4, 32, 512], P(None, 'gx', 'gy', 'gz'), may hold values from -4 to 4
- reaction: float32 [32, 4, 32, 512], P('gx', 'gy', 'gz'), may hold values from 10 to 100
Outputs:
- velocity_out: float32 [3, 32, 4, 32, 512], P(None, 'gx', 'gy', 'gz')
- pressure: float32 [32, 4, 32, 512], P('gx', 'gy', 'gz')
- residual: float32 [32, 4, 32, 512], P('gx', 'gy', 'gz')
All inputs are finite; a program needn't handle non-finite values.
Results may differ from a plain program's by a relative error of at most 0.007.
Values sent between devices are 32-bit elements; how exact they have to be, the bound alone decides.
A program may use at most 64 MiB of HBM per device.

v0:
```python
import jax
import jax.numpy as jnp
import numpy as np
from jax import lax
from jax.sharding import PartitionSpec as P

SUBSTEPS = 2
ITERS = 4


step_size = 0.02


def extended(block, sides, width, periodic):
    for axis, dim in sides:
        count = lax.axis_size(axis)
        forward = [(i, i + 1) for i in range(count - 1)]
        if periodic:
            forward.append((count - 1, 0))
        backward = [(target, source) for source, target in forward]
        low = lax.ppermute(
            lax.slice_in_dim(block, block.shape[dim] - width, None, axis=dim), axis, forward
        )
        high = lax.ppermute(lax.slice_in_dim(block, 0, width, axis=dim), axis, backward)
        block = jnp.concatenate([low, block, high], axis=dim)
    return block


def legendre_seven(points):
    earlier = points * 0.0 + 1.0
    current = points
    for degree in range(1, 7):
        earlier, current = (
            current,
            ((2 * degree + 1) * points * current - degree * earlier) / (degree + 1),
        )
    return current


def tables():
    half = np.array([0.20929921790247888, 0.5917001814331423, 0.8717401485096066, 1.0])
    points = np.concatenate([-half[::-1], half])
    legendre = legendre_seven(points)
    weights = 2.0 / (56.0 * legendre**2)
    spacing = points[:, None] - points[None, :] + np.eye(8)
    derivative = legendre[:, None] / legendre[None, :] / spacing * (1.0 - np.eye(8))
    derivative[0, 0] = -14.0
    derivative[7, 7] = 14.0
    return (jnp.asarray(weights, jnp.float32), jnp.asarray(derivative, jnp.float32))


def derive(values, derivative, along_dim, transposed):
    layout = values.shape
    matrix = derivative.T if transposed else derivative
    blocks = values.reshape(-1, 8, 8, 8)
    patterns = ("aq,nqbc->nabc", "bq,naqc->nabc", "cq,nabq->nabc")
    result = jnp.einsum(patterns[along_dim], matrix, blocks, precision=lax.Precision.HIGHEST)
    return result.reshape(layout)


def place_face(values, target_axis, position, update):
    selector = tuple(
        (position if place == target_axis else slice(None) for place in range(values.ndim))
    )
    return values.at[selector].set(update)


def faces_along_x(sequence):
    return extended(sequence, (("gx", 0),), 1, True)


def faces_along_y(sequence):
    return extended(sequence, (("gy", 0),), 1, False)


def faces_along_z(sequence):
    return extended(sequence, (("gz", 0),), 1, False)


def join_faces(values, along_dim, exchanger):
    lower_face = jnp.moveaxis(jnp.take(values, 0, axis=4 + along_dim), 1 + along_dim, 0)
    upper_face = jnp.moveaxis(jnp.take(values, 7, axis=4 + along_dim), 1 + along_dim, 0)
    elements = lower_face.shape[0]
    face_shape = lower_face.shape
    sequence = jnp.stack([lower_face, upper_face], axis=1).reshape(2 * elements, -1)
    padded = exchanger(sequence)
    paired = padded.reshape(elements + 1, 2, -1)
    totals = paired[:, 0] + paired[:, 1]
    new_lower = jnp.moveaxis(totals[:-1].reshape(face_shape), 0, 1 + along_dim)
    new_upper = jnp.moveaxis(totals[1:].reshape(face_shape), 0, 1 + along_dim)
    values = place_face(values, 4 + along_dim, 0, new_lower)
    return place_face(values, 4 + along_dim, 7, new_upper)


def assemble(values):
    exchangers = (faces_along_x, faces_along_y, faces_along_z)
    dim_order = (0, 1, 2)
    for along_dim in dim_order:
        values = join_faces(values, along_dim, exchangers[along_dim])
    return values


def dim_factors(local_count, offset, total_count, bounded_by_walls):
    element_ids = offset + jnp.arange(local_count)
    node_ids = jnp.arange(8)
    at_end = (node_ids[None, :] == 0) | (node_ids[None, :] == 7)
    low_wall = (element_ids[:, None] == 0) & (node_ids[None, :] == 0)
    high_wall = (element_ids[:, None] == total_count - 1) & (node_ids[None, :] == 7)
    on_wall = (low_wall | high_wall) & bounded_by_walls
    shared = at_end & jnp.logical_not(on_wall)
    return (jnp.where(shared, 2.0, 1.0).astype(jnp.float32), on_wall.astype(jnp.float32))


def body(velocity, reaction):
    weights, derivative = tables()
    count_x, count_y, count_z = (reaction.shape[0], reaction.shape[1], reaction.shape[2])
    speed = velocity.reshape(3, count_x, count_y, count_z, 8, 8, 8)
    react = reaction.reshape(1, count_x, count_y, count_z, 8, 8, 8)
    mass_matrix = weights[:, None, None] * weights[None, :, None] * weights[None, None, :]
    factor_x, wall_x = dim_factors(
        count_x, lax.axis_index("gx") * count_x, lax.axis_size("gx") * count_x, False
    )
    factor_y, wall_y = dim_factors(
        count_y, lax.axis_index("gy") * count_y, lax.axis_size("gy") * count_y, True
    )
    factor_z, wall_z = dim_factors(
        count_z, lax.axis_index("gz") * count_z, lax.axis_size("gz") * count_z, True
    )
    multiplicity = (
        factor_x[None, :, None, None, :, None, None]
        * factor_y[None, None, :, None, None, :, None]
        * factor_z[None, None, None, :, None, None, :]
    )
    interior = (1.0 - wall_y[None, None, :, None, None, :, None]) * (
        1.0 - wall_z[None, None, None, :, None, None, :]
    )
    stiff_sum = jnp.sum(weights[:, None] * derivative * derivative, axis=0)
    diag_local = (
        stiff_sum[:, None, None] * weights[None, :, None] * weights[None, None, :]
        + weights[:, None, None] * stiff_sum[None, :, None] * weights[None, None, :]
        + weights[:, None, None] * weights[None, :, None] * stiff_sum[None, None, :]
    )
    diag_terms = diag_local + react * mass_matrix
    speed = assemble(speed) / multiplicity
    diagonal = None
    for substep in range(SUBSTEPS):
        gradient_fields = [derive(speed, derivative, along_dim, False) for along_dim in range(3)]
        transport = (
            speed[0:1] * gradient_fields[0]
            + speed[1:2] * gradient_fields[1]
            + speed[2:3] * gradient_fields[2]
        )
        tendency = assemble(mass_matrix * transport) / (mass_matrix * multiplicity)
        speed = interior * (speed - step_size * tendency)
    spread = (
        derive(speed[0:1], derivative, 0, False)
        + derive(speed[1:2], derivative, 1, False)
        + derive(speed[2:3], derivative, 2, False)
    )
    source = -assemble(mass_matrix * spread)
    diagonal = assemble(diag_terms)

    def local_inner(first, second):
        return jnp.sum(first * second / multiplicity)

    def norm_weighted_mass(residual_vec, precond_vec):
        return lax.psum(local_inner(residual_vec, precond_vec), ("gx", "gy", "gz"))

    pressure = jnp.zeros_like(source)
    residual = source
    precond = residual / diagonal
    search = precond
    progress = norm_weighted_mass(residual, precond)
    for sweep_index in range(ITERS):
        local_sum = react * mass_matrix * search
        for apply_along_dim in range(3):
            local_sum = local_sum + derive(
                mass_matrix * derive(search, derivative, apply_along_dim, False),
                derivative,
                apply_along_dim,
                True,
            )
        applied = assemble(local_sum)
        step_length = progress / lax.psum(local_inner(search, applied), ("gx", "gy", "gz"))
        pressure = pressure + step_length * search
        residual = residual - step_length * applied
        precond = residual / diagonal
        progress_next = norm_weighted_mass(residual, precond)
        search = precond + progress_next / progress * search
        progress = progress_next
    return (
        speed.reshape(3, count_x, count_y, count_z, 512),
        pressure.reshape(count_x, count_y, count_z, 512),
        residual.reshape(count_x, count_y, count_z, 512),
    )


def solution(mesh):
    in_specs = (P(None, "gx", "gy", "gz", None), P("gx", "gy", "gz", None))
    out_specs = (
        P(None, "gx", "gy", "gz", None),
        P("gx", "gy", "gz", None),
        P("gx", "gy", "gz", None),
    )
    return jax.shard_map(body, mesh=mesh, in_specs=in_specs, out_specs=out_specs, check_vma=False)
```

profile of v0, /device:TPU:1, one launch (start us, length us, event | category | flops | bytes accessed | tf_op | source)
XLA Modules:
  0.0 1127.1 jit_solution(3727668878768256225)
XLA Ops:
  2.1 4.5 collective-permute-start
  6.6 6.2 collective-permute-start.1
  15.8 9.7 collective-permute-start.25
  30.0 4.0 collective-permute-start.2
  54.8 15.4 %scatter.189 = f32[3,2,1,4,8,8,8]{6,5,4,3,1,0,2:T(8,128)S(1)} dynamic-update-slice(f32[3,2,1,4,8,8,8]{6,5,4,3,1,0,2:T(8,128)S(1)} %scatter.186, f32[3,2,1,4,8,8,1]{6,5,4,3,1,0,2:T(8,128)S(1)} %copy.186, s32[]{:T(128)} %constant.1319.clone.1, s32[]{:T(128)} %constant.1319.clone.1, s32[]{:T(128)} %constant.1319.clone.1, s32[]{:T(128)} %constant.1319.clone.1, s32[]{:T(128)} %constant.1319.clone.1, ...) | dynamic-update-slice | bytes 12292 | tf_op jit(solution)/shard_map/scatter | solution.py:65
  81.6 12.9 %collective-permute-start.7 = (f32[1,768]{1,0:T(1,128)S(1)}, f32[1,768]{1,0:T(1,128)S(1)}, u32[]{:S(2)}, u32[]{:S(2)}) collective-permute-start(f32[1,768]{1,0:T(1,128)S(1)} %get-tuple-element.938), channel_id=1, source_target_pairs={{32,0},{64,32},{96,64},{128,96},{160,128},{192,160},{224,192},{256... | collective-permute-start | bytes 9224 | tf_op jit(solution)/shard_map/ppermute | solution.py:24
  109.1 4.0 collective-permute-start.10
  114.5 4.7 collective-permute-done.11
  127.5 15.4 %scatter.199 = f32[3,2,1,4,8,8,8]{6,5,4,3,1,0,2:T(8,128)S(1)} dynamic-update-slice(f32[3,2,1,4,8,8,8]{6,5,4,3,1,0,2:T(8,128)S(1)} %scatter.196, f32[3,2,1,4,8,8,1]{6,5,4,3,1,0,2:T(8,128)S(1)} %copy.203, s32[]{:T(128)} %constant.1319.clone.1, s32[]{:T(128)} %constant.1319.clone.1, s32[]{:T(128)} %constant.1319.clone.1, s32[]{:T(128)} %constant.1319.clone.1, s32[]{:T(128)} %constant.1319.clone.1, ...) | dynamic-update-slice | bytes 12292 | tf_op jit(solution)/shard_map/scatter | solution.py:65
  152.4 12.7 %collective-permute-start.13 = (f32[1,768]{1,0:T(1,128)S(1)}, f32[1,768]{1,0:T(1,128)S(1)}, u32[]{:S(2)}, u32[]{:S(2)}) collective-permute-start(f32[1,768]{1,0:T(1,128)S(1)} %get-tuple-element.930), channel_id=1, source_target_pairs={{32,0},{64,32},{96,64},{128,96},{160,128},{192,160},{224,192},{256... | collective-permute-start | bytes 9224 | tf_op jit(solution)/shard_map/ppermute | solution.py:24
  165.2 4.8 collective-permute-start.28
  185.1 4.3 collective-permute-start.16
  199.0 15.4 %scatter.209 = f32[3,2,1,4,8,8,8]{6,5,4,3,1,0,2:T(8,128)S(1)} dynamic-update-slice(f32[3,2,1,4,8,8,8]{6,5,4,3,1,0,2:T(8,128)S(1)} %scatter.206, f32[3,2,1,4,8,8,1]{6,5,4,3,1,0,2:T(8,128)S(1)} %copy.220, s32[]{:T(128)} %constant.1319.clone.1, s32[]{:T(128)} %constant.1319.clone.1, s32[]{:T(128)} %constant.1319.clone.1, s32[]{:T(128)} %constant.1319.clone.1, s32[]{:T(128)} %constant.1319.clone.1, ...) | dynamic-update-slice | bytes 12292 | tf_op jit(solution)/shard_map/scatter | solution.py:65
  219.2 12.8 %collective-permute-start.19 = (f32[1,256]{1,0:T(1,128)S(1)}, f32[1,256]{1,0:T(1,128)S(1)}, u32[]{:S(2)}, u32[]{:S(2)}) collective-permute-start(f32[1,256]{1,0:T(1,128)S(1)} %get-tuple-element.992), channel_id=1, source_target_pairs={{32,0},{64,32},{96,64},{128,96},{160,128},{192,160},{224,192},{256... | collective-permute-start | bytes 3080 | tf_op jit(solution)/shard_map/ppermute | solution.py:24
  246.7 4.6 scatter.229
  252.8 4.8 scatter.219
  263.0 11.8 %collective-permute-start.31 = (f32[1,256]{1,0:T(1,128)S(1)}, f32[1,256]{1,0:T(1,128)S(1)}, u32[]{:S(2)}, u32[]{:S(2)}) collective-permute-start(f32[1,256]{1,0:T(1,128)S(1)} %get-tuple-element.986), channel_id=1, source_target_pairs={{32,0},{64,32},{96,64},{128,96},{160,128},{192,160},{224,192},{256... | collective-permute-start | bytes 3080 | tf_op jit(solution)/shard_map/ppermute | solution.py:24
  283.2 4.3 collective-permute-start.34
  293.7 4.6 scatter.239
  299.1 107.2 %all-reduce = (f32[]{:T(128)}, f32[]{:T(128)}) all-reduce(f32[]{:T(128)} %get-tuple-element.811, f32[]{:T(128)} %get-tuple-element.810), channel_id=1, replica_groups=mesh['gx'=16,'gy'=4,'gz'=8] {'gx','gy','gz'}, use_global_device_ids=true, to_apply=%region_2.15 | all-reduce | flops 2 | bytes 16 | tf_op jit(solution)/shard_map/psum | solution.py:167
  408.4 94.4 %psum.58 = f32[]{:T(128)} all-reduce(f32[]{:T(128)} %get-tuple-element.862), channel_id=1, replica_groups=mesh['gx'=16,'gy'=4,'gz'=8] {'gx','gy','gz'}, use_global_device_ids=true, to_apply=%region_6.19 | all-reduce | flops 1 | bytes 8 | tf_op jit(solution)/shard_map/psum | solution.py:167
  507.7 4.2 collective-permute-start.36
  535.5 4.6 scatter.249
  540.9 104.3 %psum.59 = f32[]{:T(128)} all-reduce(f32[]{:T(128)} %fusion.31), channel_id=1, replica_groups=mesh['gx'=16,'gy'=4,'gz'=8] {'gx','gy','gz'}, use_global_device_ids=true, to_apply=%region_8.21 | all-reduce | flops 1 | bytes 8 | tf_op jit(solution)/shard_map/psum | solution.py:184
  647.9 94.4 %psum.60 = f32[]{:T(128)} all-reduce(f32[]{:T(128)} %get-tuple-element.859), channel_id=1, replica_groups=mesh['gx'=16,'gy'=4,'gz'=8] {'gx','gy','gz'}, use_global_device_ids=true, to_apply=%region_10.23 | all-reduce | flops 1 | bytes 8 | tf_op jit(solution)/shard_map/psum | solution.py:167
  747.1 4.2 collective-permute-start.42
  774.1 4.6 scatter.259
  779.5 103.8 %psum.61 = f32[]{:T(128)} all-reduce(f32[]{:T(128)} %fusion.33), channel_id=1, replica_groups=mesh['gx'=16,'gy'=4,'gz'=8] {'gx','gy','gz'}, use_global_device_ids=true, to_apply=%region_12.25 | all-reduce | flops 1 | bytes 8 | tf_op jit(solution)/shard_map/psum | solution.py:184
  886.0 94.7 %psum.62 = f32[]{:T(128)} all-reduce(f32[]{:T(128)} %get-tuple-element.856), channel_id=1, replica_groups=mesh['gx'=16,'gy'=4,'gz'=8] {'gx','gy','gz'}, use_global_device_ids=true, to_apply=%region_14.27 | all-reduce | flops 1 | bytes 8 | tf_op jit(solution)/shard_map/psum | solution.py:167
  985.5 4.2 collective-permute-start.48
  1012.5 4.6 scatter.269
  1018.9 103.9 %psum.63 = f32[]{:T(128)} all-reduce(f32[]{:T(128)} %fusion.35), channel_id=1, replica_groups=mesh['gx'=16,'gy'=4,'gz'=8] {'gx','gy','gz'}, use_global_device_ids=true, to_apply=%region_16.29 | all-reduce | flops 1 | bytes 8 | tf_op jit(solution)/shard_map/psum | solution.py:184
  (563 shorter events, 227.0 us)
Async XLA Ops:
  2.1 27.2 %collective-permute-start = (f32[1,768]{1,0:T(1,128)S(1)}, f32[1,768]{1,0:T(1,128)S(1)}, u32[]{:S(2)}, u32[]{:S(2)}) collective-permute-start(f32[1,768]{1,0:T(1,128)S(1)} %get-tuple-element.945), channel_id=1, source_target_pairs={{0,32},{32,64},{64,96},{96,128},{128,160},{160,192},{192,224},{224... | collective-permute-start | bytes 9224 | tf_op jit(solution)/shard_map/ppermute | solution.py:21
  6.6 22.7 %collective-permute-start.1 = (f32[1,768]{1,0:T(1,128)S(1)}, f32[1,768]{1,0:T(1,128)S(1)}, u32[]{:S(2)}, u32[]{:S(2)}) collective-permute-start(f32[1,768]{1,0:T(1,128)S(1)} %get-tuple-element.946), channel_id=1, source_target_pairs={{32,0},{64,32},{96,64},{128,96},{160,128},{192,160},{224,192},{256... | collective-permute-start | bytes 9224 | tf_op jit(solution)/shard_map/ppermute | solution.py:24
  13.9 12.1 %collective-permute-start.24 = (f32[1,256]{1,0:T(1,128)S(1)}, f32[1,256]{1,0:T(1,128)S(1)}, u32[]{:S(2)}, u32[]{:S(2)}) collective-permute-start(f32[1,256]{1,0:T(1,128)S(1)} %get-tuple-element.997), channel_id=1, source_target_pairs={{0,32},{32,64},{64,96},{96,128},{128,160},{160,192},{192,224},{224... | collective-permute-start | bytes 3080 | tf_op jit(solution)/shard_map/ppermute | solution.py:21
  15.8 10.5 collective-permute-start.25
  26.7 8.7 collective-permute-start.26
  28.1 7.3 collective-permute-start.27
  30.0 5.5 collective-permute-start.2
  79.4 15.9 %collective-permute-start.6 = (f32[1,768]{1,0:T(1,128)S(1)}, f32[1,768]{1,0:T(1,128)S(1)}, u32[]{:S(2)}, u32[]{:S(2)}) collective-permute-start(f32[1,768]{1,0:T(1,128)S(1)} %get-tuple-element.937), channel_id=1, source_target_pairs={{0,32},{32,64},{64,96},{96,128},{128,160},{160,192},{192,224},{224... | collective-permute-start | bytes 9224 | tf_op jit(solution)/shard_map/ppermute | solution.py:21
  81.6 13.7 %collective-permute-start.7 = (f32[1,768]{1,0:T(1,128)S(1)}, f32[1,768]{1,0:T(1,128)S(1)}, u32[]{:S(2)}, u32[]{:S(2)}) collective-permute-start(f32[1,768]{1,0:T(1,128)S(1)} %get-tuple-element.938), channel_id=1, source_target_pairs={{32,0},{64,32},{96,64},{128,96},{160,128},{192,160},{224,192},{256... | collective-permute-start | bytes 9224 | tf_op jit(solution)/shard_map/ppermute | solution.py:24
  109.1 5.4 collective-permute-start.10
  113.1 6.2 collective-permute-start.11
  150.5 20.8 %collective-permute-start.12 = (f32[1,768]{1,0:T(1,128)S(1)}, f32[1,768]{1,0:T(1,128)S(1)}, u32[]{:S(2)}, u32[]{:S(2)}) collective-permute-start(f32[1,768]{1,0:T(1,128)S(1)} %get-tuple-element.929), channel_id=1, source_target_pairs={{0,32},{32,64},{64,96},{96,128},{128,160},{160,192},{192,224},{224... | collective-permute-start | bytes 9224 | tf_op jit(solution)/shard_map/ppermute | solution.py:21
  152.4 18.9 %collective-permute-start.13 = (f32[1,768]{1,0:T(1,128)S(1)}, f32[1,768]{1,0:T(1,128)S(1)}, u32[]{:S(2)}, u32[]{:S(2)}) collective-permute-start(f32[1,768]{1,0:T(1,128)S(1)} %get-tuple-element.930), channel_id=1, source_target_pairs={{32,0},{64,32},{96,64},{128,96},{160,128},{192,160},{224,192},{256... | collective-permute-start | bytes 9224 | tf_op jit(solution)/shard_map/ppermute | solution.py:24
  165.2 11.8 %collective-permute-start.28 = (f32[1,128]{1,0:T(1,128)S(1)}, f32[1,128]{1,0:T(1,128)S(1)}, u32[]{:S(2)}, u32[]{:S(2)}) collective-permute-start(f32[1,128]{1,0:T(1,128)S(1)} %get-tuple-element.995), channel_id=1, source_target_pairs={{0,1},{1,2},{2,3},{3,4},{4,5},{5,6},{6,7},{8,9},{9,10},{10,11},{11... | collective-permute-start | bytes 1544 | tf_op jit(solution)/shard_map/ppermute | solution.py:21
  170.0 7.0 collective-permute-start.29
  185.1 5.6 collective-permute-start.16
  217.2 14.7 %collective-permute-start.18 = (f32[1,256]{1,0:T(1,128)S(1)}, f32[1,256]{1,0:T(1,128)S(1)}, u32[]{:S(2)}, u32[]{:S(2)}) collective-permute-start(f32[1,256]{1,0:T(1,128)S(1)} %get-tuple-element.991), channel_id=1, source_target_pairs={{0,32},{32,64},{64,96},{96,128},{128,160},{160,192},{192,224},{224... | collective-permute-start | bytes 3080 | tf_op jit(solution)/shard_map/ppermute | solution.py:21
  219.2 13.6 %collective-permute-start.19 = (f32[1,256]{1,0:T(1,128)S(1)}, f32[1,256]{1,0:T(1,128)S(1)}, u32[]{:S(2)}, u32[]{:S(2)}) collective-permute-start(f32[1,256]{1,0:T(1,128)S(1)} %get-tuple-element.992), channel_id=1, source_target_pairs={{32,0},{64,32},{96,64},{128,96},{160,128},{192,160},{224,192},{256... | collective-permute-start | bytes 3080 | tf_op jit(solution)/shard_map/ppermute | solution.py:24
  240.3 11.0 collective-permute-start.22
  243.9 7.4 collective-permute-start.23
  261.1 13.8 %collective-permute-start.30 = (f32[1,256]{1,0:T(1,128)S(1)}, f32[1,256]{1,0:T(1,128)S(1)}, u32[]{:S(2)}, u32[]{:S(2)}) collective-permute-start(f32[1,256]{1,0:T(1,128)S(1)} %get-tuple-element.985), channel_id=1, source_target_pairs={{0,32},{32,64},{64,96},{96,128},{128,160},{160,192},{192,224},{224... | collective-permute-start | bytes 3080 | tf_op jit(solution)/shard_map/ppermute | solution.py:21
  263.0 12.7 %collective-permute-start.31 = (f32[1,256]{1,0:T(1,128)S(1)}, f32[1,256]{1,0:T(1,128)S(1)}, u32[]{:S(2)}, u32[]{:S(2)}) collective-permute-start(f32[1,256]{1,0:T(1,128)S(1)} %get-tuple-element.986), channel_id=1, source_target_pairs={{32,0},{64,32},{96,64},{128,96},{160,128},{192,160},{224,192},{256... | collective-permute-start | bytes 3080 | tf_op jit(solution)/shard_map/ppermute | solution.py:24
  283.2 5.6 collective-permute-start.34
  507.7 6.2 collective-permute-start.36
  511.9 5.2 collective-permute-start.37
  517.5 5.3 collective-permute-start.38
  747.1 6.2 collective-permute-start.42
  751.4 5.2 collective-permute-start.43
  767.4 5.2 collective-permute-start.47
  985.5 6.2 collective-permute-start.48
  989.7 5.2 collective-permute-start.49
  1005.8 5.2 collective-permute-start.53
  (30 other events, 211.7 us)
where the time goes:
time: 1140 us; the launch traced here: 1130 us
  blocking collectives  703 us (62%)
  starting transfers between devices  176 us (15%)
  local copies, waits for them, and re-layouts  148 us (13%)
  waiting for transfers between devices  60.7 us (5%)
  matrix products  17.8 us (2%)
  between operations  13.6 us (1%)
    psum x4, blocking collectives, norm_weighted_mass(): return lax.psum(local_inner(residual_vec, precond_vec), ('gx', 'gy', 'gz'))  391 us
    psum x3, blocking collectives, body(): lax.psum(local_inner(search, applied), ('gx', 'gy', 'gz'))  312 us
    scatter x54, local copies, waits for them, and re-layouts, place_face(): return values.at[selector].set(update)  98.6 us
    ppermute x27, starting transfers between devices, extended(): lax.ppermute(lax.slice_in_dim(block, 0, width, axis=dim), axis, backward)  95.5 us
    ppermute x27, starting transfers between devices, extended(): lax.ppermute(lax.slice_in_dim(block, block.shape[dim] - width, None, axis...  80.1 us
    ppermute x27, waiting for transfers between devices, extended(): lax.ppermute(lax.slice_in_dim(block, 0, width, axis=dim), axis, backward)  60.7 us
  transfers between devices with their start and end apart: 54, of which 21 were waited for; matrix products, arithmetic and copies ran while one was open for 1% of the time, Pallas kernels for 0%

commit v1 on v0

v1 whole, which is shorter than its diff:
```python
import jax
import jax.numpy as jnp
import numpy as np
from jax import lax
from jax.experimental import pallas as pl
from jax.experimental.pallas import tpu as pltpu
from jax.sharding import PartitionSpec as P

MESH = pl.DeviceIdType.MESH
STEP = 0.02
HALF = 64
OFFSETS = ((-1, 0), (1, 0), (0, -1), (0, 1), (-1, -1), (1, -1), (-1, 1), (1, 1))
ROUND_FIELDS = (4, 3, 3, 1, 1, 1, 1, 1)


def roll(values, shift, axis):
    shift = shift % values.shape[axis]
    return values if shift == 0 else pltpu.roll(values, shift, axis)


def div(value, by):
    return value // by if isinstance(value, (int, np.ndarray)) else lax.div(value, np.int32(by))


def rem(value, by):
    return value % by if isinstance(value, (int, np.ndarray)) else lax.rem(value, np.int32(by))


def tables():
    half = np.array([0.2092992179024788687, 0.5917001814331423022, 0.8717401485096066153, 1.0])
    points = np.concatenate([-half[::-1], half])
    earlier, current = points * 0.0 + 1.0, points
    for degree in range(1, 7):
        earlier, current = current, ((2 * degree + 1) * points * current - degree * earlier) / (degree + 1)
    w = 2.0 / (56.0 * current**2)
    spacing = points[:, None] - points[None, :] + np.eye(8)
    d = current[:, None] / current[None, :] / spacing * (1.0 - np.eye(8))
    d[0, 0] = -14.0
    d[7, 7] = 14.0
    k = d.T @ np.diag(w) @ d
    lane = np.arange(128)
    c, b, a_lo = lane % 8, (lane // 8) % 8, lane // 64
    rows = {}

    def put(name, values):
        rows[name] = (len(stack), len(values))
        stack.extend(values)

    stack = []

    def along_a(matrix, scale):
        return [matrix[2 * j + a_lo, q] * scale for j in range(4) for q in range(8)]

    def shifts(matrix, index, scale):
        out = []
        for s in range(-7, 8):
            source = index - s
            inside = (source >= 0) & (source <= 7)
            out.append(np.where(inside, matrix[index, np.clip(source, 0, 7)], 0.0) * scale)
        return out

    one = np.ones(128)
    put("da", along_a(d, one))
    put("db", shifts(d, b, one))
    put("dc", shifts(d, c, one))
    put("ka", along_a(k, w[b] * w[c]))
    put("kb", shifts(k, b, w[c]))
    put("kc", shifts(k, c, w[b]))
    put("wa", [w[2 * i + a_lo] for i in range(4)])
    mass = [w[2 * i + a_lo] * w[b] * w[c] for i in range(4)]
    put("mass", mass)
    put("tend", [STEP / m for m in mass])
    s = (w[:, None] * d * d).sum(0)
    put("diag", [s[2 * i + a_lo] * w[b] * w[c] + w[2 * i + a_lo] * s[b] * w[c] + w[2 * i + a_lo] * w[b] * s[c] for i in range(4)])
    table = np.stack(stack).astype(np.float32)
    return np.ascontiguousarray(np.broadcast_to(table[:, None, :], (len(stack), 8, 128))), rows


TABLE, ROWS = tables()


def owner_of(axial, depth):
    y, core = div(axial, 2), rem(axial, 2)
    z, turn = div(depth, 4), rem(depth, 4)
    x = turn + rem(z, 2) * (3 - 2 * turn)
    return (div(y, 4) * 8 + x * 2 + core, rem(y, 4), z)


class Place:
    def __init__(self, gx, gy, gz):
        self.gx, self.gy, self.gz = gx, gy, gz
        self.core, self.x, self.y_hi = rem(gx, 2), rem(div(gx, 2), 4), div(gx, 8)
        self.y, self.z = self.y_hi * 4 + gy, gz
        self.axial = self.y * 2 + self.core
        self.turn = self.x + rem(gz, 2) * (3 - 2 * self.x)
        self.depth = self.z * 4 + self.turn

    def mesh_id(self, x, y, z, core):
        return (div(y, 4) * 8 + x * 2 + core, rem(y, 4), z)

    def neighbour(self, dx, dz):
        return owner_of(rem(self.axial + dx + 16, 16), rem(self.depth + dz + 32, 32))

    def worker(self, i):
        x = rem(self.x + i, 4)
        return self.mesh_id(x, self.y_hi * 4 + self.x, self.z, self.core), x + rem(self.z, 2) * (3 - 2 * x)

    def home(self, i):
        cross = rem(self.gy + i, 4)
        return self.mesh_id(self.gy, self.y_hi * 4 + cross, self.z, self.core), cross

    def group(self, stage, i):
        if stage == 0:
            me = self.x * 2 + self.core
            other = rem(me + i, 8)
            return self.mesh_id(div(other, 2), self.y, self.z, rem(other, 2)), me
        if stage == 1:
            return self.mesh_id(self.x, rem(self.y + i, 8), self.z, self.core), self.y
        return self.mesh_id(self.x, self.y, rem(self.z + i, 8), self.core), self.z


class Masks:
    def __init__(self, depth):
        lane = lax.broadcasted_iota(jnp.int32, (8, 128), 1)
        row = lax.broadcasted_iota(jnp.int32, (8, 128), 0)
        c, b = lane & 7, (lane >> 3) & 7
        cross = row >> 1
        self.low = lane < HALF
        self.even = (row & 1) == 0
        odd = (row & 1) == 1
        high = lane >= HALF
        self.b0 = (b == 0) & (cross > 0)
        self.b7 = (b == 7) & (cross < 3)
        self.in0 = odd & self.low
        self.in3 = self.even & high
        self.out0 = self.even & self.low
        self.out3 = odd & high
        self.c = c
        self.c0, self.c7 = c == 0, c == 7
        self.slot_low = c < 4
        self.edge0 = self.out0 & ((c & 3) == 0)
        self.edge3 = self.out3 & ((c & 3) == 3)
        up = (depth < 31).astype(jnp.float32)
        down = (depth > 0).astype(jnp.float32)
        self.zmask = jnp.where(self.slot_low, up, down)
        one = jnp.ones((8, 128), jnp.float32)
        iy = jnp.where(self.b0 | self.b7, 0.5, one)
        iz = jnp.where(self.c0, 1.0 - 0.5 * down, jnp.where(self.c7, 1.0 - 0.5 * up, one))
        iyz = iy * iz
        self.inverse = [iyz * jnp.where(self.low, 0.5, one), iyz, iyz, iyz * jnp.where(self.low, one, 0.5)]
        wall_y = ((b == 0) & (cross == 0)) | ((b == 7) & (cross == 3))
        self.interior = jnp.where(wall_y, 0.0, jnp.where(self.c0, down, jnp.where(self.c7, up, one)))


def join_block(v, m):
    out = []
    for x in v:
        g = roll(roll(x, 2, 1), -56, 2)
        h = roll(roll(x, -2, 1), 56, 2)
        out.append(x + jnp.where(m.b0, g, jnp.where(m.b7, h, 0.0)))
    first = roll(roll(out[3], 1, 1), HALF, 2)
    last = roll(roll(out[0], -1, 1), HALF, 2)
    out[0] = out[0] + jnp.where(m.in0, first, 0.0)
    out[3] = out[3] + jnp.where(m.in3, last, 0.0)
    return out


def pack(v, m):
    axial = jnp.where(m.low, v[0], v[3])
    depth = v[0]
    for i in range(1, 4):
        depth = jnp.where(m.c == i, roll(v[i], i, 2), depth)
    for i in range(4):
        depth = jnp.where(m.c == 4 + i, roll(v[i], i - 3, 2), depth)
    return axial, depth


def unpack(v, got, m):
    v = list(v)
    v[0] = v[0] + jnp.where(m.out0, roll(roll(got[0], -1, 1), HALF, 2), 0.0)
    v[3] = v[3] + jnp.where(m.out3, roll(roll(got[1], 1, 1), HALF, 2), 0.0)
    centre = jnp.where(m.slot_low, got[3], got[2])
    before = jnp.where(m.slot_low, got[6], got[4])
    after = jnp.where(m.slot_low, got[7], got[5])
    face = centre + jnp.where(m.edge0, roll(roll(before, -1, 1), -67, 2), 0.0)
    face = face + jnp.where(m.edge3, roll(roll(after, 1, 1), 67, 2), 0.0)
    face = face * m.zmask
    return [
        v[i] + jnp.where(m.c7, roll(face, 7 - i, 2), jnp.where(m.c0, roll(face, -4 - i, 2), 0.0))
        for i in range(4)
    ]


def along_a(v, get, name, m):
    parts = []
    for x in v:
        turned = roll(x, HALF, 2)
        parts.append(jnp.where(m.low, x, turned))
        parts.append(jnp.where(m.low, turned, x))
    start = ROWS[name][0]
    return [sum_of([get(start + j * 8 + q) * parts[q] for q in range(8)]) for j in range(4)]


def along_lanes(v, get, name, stride):
    start = ROWS[name][0]
    return [sum_of([get(start + s + 7) * roll(x, s * stride, 2) for s in range(-7, 8)]) for x in v]


def sum_of(terms):
    while len(terms) > 1:
        terms = [terms[i] + terms[i + 1] if i + 1 < len(terms) else terms[i] for i in range(0, len(terms), 2)]
    return terms[0]


def constant(get, name):
    return [get(ROWS[name][0] + i) for i in range(4)]


def transport(u, get, m):
    da = along_a(u, get, "da", m)
    db = along_lanes(u, get, "db", 8)
    dc = along_lanes(u, get, "dc", 1)
    mass = constant(get, "mass")
    return [mass[i] * (u[i][0:1] * da[i] + u[i][1:2] * db[i] + u[i][2:3] * dc[i]) for i in range(4)]


def divergence(u, get, m):
    da = along_a([x[0:1] for x in u], get, "da", m)
    db = along_lanes([x[1:2] for x in u], get, "db", 8)
    dc = along_lanes([x[2:3] for x in u], get, "dc", 1)
    mass = constant(get, "mass")
    return [-mass[i] * (da[i] + db[i] + dc[i]) for i in range(4)]


def stiffness(p, scaled, get, m):
    ka = along_a(p, get, "ka", m)
    kb = along_lanes(p, get, "kb", 8)
    kc = along_lanes(p, get, "kc", 1)
    wa = constant(get, "wa")
    return [ka[i] + wa[i] * (kb[i] + kc[i]) + scaled[i] * p[i] for i in range(4)]


def moment(f, g, weight=None):
    total = sum_of([f[i][0] * g[i][0] if weight is None else f[i][0] * g[i][0] * weight[i] for i in range(4)])
    return jnp.sum(total, axis=0, keepdims=True)


def solve(n, e):
    g = [[(n[i + j] + n[i + j + 1]) if i + j < 6 else e for j in range(4)] for i in range(4)]
    rhs = [n[i] for i in range(4)]
    inverse = []
    for i in range(4):
        inverse.append(1.0 / g[i][i])
        for r in range(i + 1, 4):
            factor = g[r][i] * inverse[i]
            for j in range(i + 1, 4):
                g[r][j] = g[r][j] - factor * g[i][j]
            rhs[r] = rhs[r] - factor * rhs[i]
    out = [None] * 4
    for i in range(3, -1, -1):
        total = rhs[i]
        for j in range(i + 1, 4):
            total = total - g[i][j] * out[j]
        out[i] = total * inverse[i]
    return out


def kernel(vel_hbm, react_hbm, table_hbm, velo_ref, press_ref, resid_ref, vel, react, tab, load_sem,
           send0, recv0, sem0, *rest):
    rounds = len(ROUND_FIELDS)
    send_x, send_z = rest[0:rounds], rest[rounds:2 * rounds]
    got_refs = rest[2 * rounds:3 * rounds]
    (round_sem, sums, part, sum_sem, back_send, back_recv, back_sem, scratch) = rest[3 * rounds:]
    place = Place(lax.axis_index("gx"), lax.axis_index("gy"), lax.axis_index("gz"))

    def push(pairs, device, send_sem, recv_sem, own=None):
        def remote():
            for source, target in pairs:
                pltpu.make_async_remote_copy(source, target, send_sem, recv_sem,
                                             device_id=device, device_id_type=MESH).start()

        if own is None:
            remote()
            return
        pl.when(jnp.logical_not(own))(remote)

        @pl.when(own)
        def _():
            for source, target in pairs:
                pltpu.make_async_copy(source, target, recv_sem).start()

    def greet(device):
        pl.semaphore_signal(barrier, inc=1, device_id=device, device_id_type=MESH)

    barrier = pltpu.get_barrier_semaphore()
    count = 0
    for i in range(4):
        greet(place.worker(i)[0])
        greet(place.home(i)[0])
        count += 2
    for dx, dz in OFFSETS:
        greet(place.neighbour(dx, dz))
        count += 1
    for stage in range(3):
        for i in range(1, 8):
            greet(place.group(stage, i)[0])
            count += 1

    loads = [pltpu.make_async_copy(s, d, load_sem.at[k]) for k, (s, d) in
             enumerate(((vel_hbm, vel), (react_hbm, react), (table_hbm, tab)))]
    for copy in loads:
        copy.start()
    m = Masks(place.depth)
    loads[0].wait()
    loads[1].wait()
    for f in range(4):
        for x in range(2):
            for i in range(4):
                lanes = slice(i * 128, (i + 1) * 128)
                piece = vel[2 * f + x, :, lanes] if f < 3 else react[x, :, lanes]
                send0[pl.ds(f * 8 + x * 4 + i, 4, stride=32), :] = piece
    pl.semaphore_wait(barrier, count)

    own = place.x == place.gy
    into = pl.ds(pl.multiple_of(place.gy * 8, 8), 8)
    for i in range(4):
        device, turn = place.worker(i)
        pairs = [(send0.at[pl.ds(pl.multiple_of(turn * 32 + f * 8, 8), 8)], recv0.at[f, into]) for f in range(4)]
        push(pairs, device, sem0.at[i], sem0.at[4], None if i else own)

    loads[2].wait()

    def get(row):
        return tab[row]

    pltpu.make_async_copy(recv0, recv0, sem0.at[4]).wait()
    fields = [jnp.stack([recv0[f, pl.ds(i, 8, stride=4), :] for f in range(4)]) for i in range(4)]

    def begin(r, v):
        v = join_block(v, m)
        axial, depth = pack(v, m)
        send_x[r][...] = axial
        send_z[r][...] = depth
        for k, (dx, dz) in enumerate(OFFSETS):
            slot = OFFSETS.index((-dx, -dz))
            pltpu.make_async_remote_copy(
                send_x[r] if dz == 0 else send_z[r], got_refs[r].at[slot],
                round_sem.at[0, r], round_sem.at[1, r],
                device_id=place.neighbour(dx, dz), device_id_type=MESH).start()
        return v

    def finish(r, v):
        pltpu.make_async_copy(got_refs[r], got_refs[r], round_sem.at[1, r]).wait()
        return unpack(v, [got_refs[r][k] for k in range(8)], m)

    def assemble(r, v):
        return finish(r, begin(r, v))

    groups = ((0, 4), (4, 3), (7, 1), (8, 1))

    def give_back(g):
        first, number = groups[g]
        into = pl.ds(pl.multiple_of(place.turn * 8, 8), 8)
        for i in range(4):
            device, cross = place.home(i)
            rows = pl.ds(pl.multiple_of(cross * 8, 8), 8)
            pairs = [(back_send.at[f, rows], back_recv.at[f, into]) for f in range(first, first + number)]
            push(pairs, device, back_sem.at[i, g], back_sem.at[4, g], None if i else own)

    def returned(g):
        first, number = groups[g]
        ref = back_recv.at[pl.ds(first, number)]
        pltpu.make_async_copy(ref, ref, back_sem.at[4, g]).wait()

    def keep(f, v):
        for i in range(4):
            back_send[f, pl.ds(i, 8, stride=4), :] = v[i]

    mass = constant(get, "mass")
    scaled = [fields[i][3:4] * mass[i] for i in range(4)]
    diag_local = constant(get, "diag")
    v = [jnp.concatenate([fields[i][0:3], scaled[i] + diag_local[i]], axis=0) for i in range(4)]
    v = assemble(0, v)
    diag = [x[3:4] for x in v]
    inverse_diag = [1.0 / x for x in diag]
    u = [v[i][0:3] * m.inverse[i] for i in range(4)]
    keep(3, [x[0] for x in diag])
    tend = constant(get, "tend")
    tend = [tend[i] * m.inverse[i] * m.interior for i in range(4)]
    for r in (1, 2):
        t = assemble(r, transport(u, get, m))
        u = [m.interior * u[i] - tend[i] * t[i] for i in range(4)]
    for k in range(3):
        keep(k, [x[k] for x in u])
    source = begin(3, divergence(u, get, m))
    give_back(0)
    source = finish(3, source)

    q = [[source[i] * inverse_diag[i] for i in range(4)]]
    weight = [diag[i][0] * m.inverse[i] for i in range(4)]
    part[0, 0:1, :] = moment(q[0], source, m.inverse)
    keep(4, [x[0] for x in q[0]])
    for j in range(3):
        w = begin(4 + j, stiffness(q[j], scaled, get, m))
        if j == 1:
            part[0, 2:3, :] = moment(q[1], q[1], weight)
        if j == 2:
            give_back(1)
            part[0, 3:4, :] = moment(q[1], q[2], weight)
            part[0, 4:5, :] = moment(q[2], q[2], weight)
        if j == 1:
            part[0, 1:2, :] = moment(q[0], q[1], weight)
        w = finish(4 + j, w)
        q.append([w[i] * inverse_diag[i] - q[j][i] for i in range(4)])
        keep(5 + j, [x[0] for x in q[j + 1]])
    w = stiffness(q[3], scaled, get, m)
    part[0, 5:6, :] = moment(q[2], q[3], weight)
    part[0, 6:7, :] = moment(q[3], q[3], weight)
    part[0, 7:8, :] = moment(q[3], w)

    def send_sum(stage):
        for i in range(1, 8):
            device, me = place.group(stage, i)
            pltpu.make_async_remote_copy(part.at[stage], sums.at[stage, 7 - i], sum_sem.at[0, stage],
                                         sum_sem.at[1, stage], device_id=device, device_id_type=MESH).start()

    def take_sum(stage):
        pltpu.make_async_copy(sums.at[stage], sums.at[stage], sum_sem.at[1, stage]).wait()
        return sum_of([part[stage]] + [sums[stage, i] for i in range(7)])

    send_sum(0)
    w = begin(7, w)
    give_back(2)
    part[1] = take_sum(0)
    send_sum(1)
    w = finish(7, w)
    keep(8, [x[0] for x in w])
    give_back(3)

    returned(0)
    for f in range(3):
        for x in range(2):
            for i in range(4):
                velo_ref[2 * f + x, :, i * 128:(i + 1) * 128] = back_recv[f, pl.ds(x * 4 + i, 4, stride=8), :]

    part[2] = take_sum(1)
    send_sum(2)
    total = take_sum(2)
    n = jnp.broadcast_to(jnp.sum(total, axis=1, keepdims=True), (8, 128))
    c = solve([n[i:i + 1, :] for i in range(7)], n[7:8, :])

    for g in (1, 2, 3):
        returned(g)
    d, q0, q1, q2, q3, w3 = [back_recv[f] for f in range(3, 9)]
    scratch[0] = c[0] * q0 + c[1] * q1 + c[2] * q2 + c[3] * q3
    scratch[1] = d * (q0 - c[0] * (q0 + q1) - c[1] * (q1 + q2) - c[2] * (q2 + q3)) - c[3] * w3
    for f, ref in ((0, press_ref), (1, resid_ref)):
        for x in range(2):
            for i in range(4):
                ref[x, :, i * 128:(i + 1) * 128] = scratch[f, pl.ds(x * 4 + i, 4, stride=8), :]

    for r in range(rounds):
        pltpu.make_async_copy(got_refs[r], got_refs[r], round_sem.at[0, r]).wait()
    for stage in range(3):
        pltpu.make_async_copy(sums.at[stage], sums.at[stage], sum_sem.at[0, stage]).wait()

    def sent(i):
        ref = recv0.at[:, pl.ds(0, 8)]
        pltpu.make_async_copy(ref, ref, sem0.at[i]).wait()
        for g, (first, number) in enumerate(groups):
            ref = back_recv.at[pl.ds(first, number), pl.ds(0, 8)]
            pltpu.make_async_copy(ref, ref, back_sem.at[i, g]).wait()

    for i in range(1, 4):
        sent(i)

    @pl.when(jnp.logical_not(own))
    def _():
        sent(0)


def body(velocity, reaction, table):
    f32 = jnp.float32
    spec = pl.BlockSpec(memory_space=pl.ANY)
    vmem = pl.BlockSpec(memory_space=pltpu.VMEM)
    scratch = [
        pltpu.VMEM((6, 4, 512), f32), pltpu.VMEM((2, 4, 512), f32), pltpu.VMEM(table.shape, f32),
        pltpu.SemaphoreType.DMA((3,)),
        pltpu.VMEM((128, 128), f32), pltpu.VMEM((4, 32, 128), f32), pltpu.SemaphoreType.DMA((5,)),
    ]
    scratch += [pltpu.VMEM((n, 8, 128), f32) for n in ROUND_FIELDS] * 2
    scratch += [pltpu.VMEM((8, n, 8, 128), f32) for n in ROUND_FIELDS]
    scratch += [
        pltpu.SemaphoreType.DMA((2, len(ROUND_FIELDS))),
        pltpu.VMEM((3, 7, 8, 128), f32), pltpu.VMEM((3, 8, 128), f32), pltpu.SemaphoreType.DMA((2, 3)),
        pltpu.VMEM((9, 32, 128), f32), pltpu.VMEM((9, 32, 128), f32), pltpu.SemaphoreType.DMA((5, 4)),
        pltpu.VMEM((2, 32, 128), f32),
    ]
    velo, press, resid = pl.pallas_call(
        kernel,
        out_shape=[jax.ShapeDtypeStruct((6, 4, 512), f32)] + [jax.ShapeDtypeStruct((2, 4, 512), f32)] * 2,
        in_specs=[spec] * 3,
        out_specs=[vmem] * 3,
        scratch_shapes=scratch,
        compiler_params=pltpu.CompilerParams(collective_id=0, has_side_effects=True),
        name="duct_step",
    )(velocity.reshape(6, 4, 512), reaction.reshape(2, 4, 512), table)
    return velo.reshape(velocity.shape), press.reshape(reaction.shape), resid.reshape(reaction.shape)


def solution(mesh):
    specs = (P(None, "gx", "gy", "gz", None), P("gx", "gy", "gz", None))

    def step(velocity, reaction):
        return body(velocity, reaction, jnp.asarray(TABLE))

    return jax.shard_map(
        step, mesh=mesh, in_specs=specs, out_specs=(specs[0], specs[1], specs[1]), check_vma=False
    )
```

time: 1140 us -> 68.5 us (0.06); the launches traced: 1130 us -> 67.9 us
  blocking collectives: 703 us -> 0 us
  starting transfers between devices: 176 us -> 0 us
  local copies, waits for them, and re-layouts: 148 us -> 2.76 us
  Pallas kernels: 0 us -> 64.5 us
  waiting for transfers between devices: 60.7 us -> 0 us
  matrix products: 17.8 us -> 0 us
  between operations: 13.6 us -> 0.65 us
    psum x7 -> x0, blocking collectives: 703 us -> none  [the longest x4 391 us: norm_weighted_mass(): return lax.psum(local_inner(residual_vec, precond_vec), ('gx', 'gy', 'gz'))]
    ppermute x54 -> x0, starting transfers between devices: 176 us -> none  [the longest x27 95.5 us: extended(): lax.ppermute(lax.slice_in_dim(block, 0, width, axis=dim), axis, backward)]
    scatter x54 -> x0, local copies, waits for them, and re-layouts: 98.6 us -> none  [place_face(): return values.at[selector].set(update)]
    pallas_call x0 -> x1, Pallas kernels: none -> 64.5 us  [body(): pl.pallas_call(kernel, out_shape=[jax.ShapeDtypeStruct((6, 4, 512), f32)]...]
    ppermute x54 -> x0, waiting for transfers between devices: 60.7 us -> none  [the longest x27 60.7 us: extended(): lax.ppermute(lax.slice_in_dim(block, 0, width, axis=dim), axis, backward)]
    another operation x102 -> x0, local copies, waits for them, and re-layouts: 23.3 us -> none
    dot_general x33 -> x0, matrix products: 17.8 us -> none  [derive(): jnp.einsum(patterns[along_dim], matrix, blocks, precision=lax.Precision.H...]
    reshape x78 -> x0, local copies, waits for them, and re-layouts: 11.7 us -> none  [the longest x4 1.96 us: derive(): blocks = values.reshape(-1, 8, 8, 8)]
  transfers between devices with their start and end apart: 54 -> 0, of which waited for: 21 -> 0; matrix products, arithmetic and copies ran while one was open for 1% -> 0% of each run, Pallas kernels for 0% -> 0%
where the time goes in v1:
time: 68.5 us; the launch traced here: 67.9 us
  Pallas kernels  64.5 us (94%)
  local copies, waits for them, and re-layouts  2.76 us (4%)
    pallas_call x1, Pallas kernels, body(): pl.pallas_call(kernel, out_shape=[jax.ShapeDtypeStruct((6, 4, 512), f32)]...  64.5 us
    unnamed x7, local copies, waits for them, and re-layouts  2.76 us

profile of v1, /device:TPU:1, one launch (start us, length us, event | category | flops | bytes accessed | tf_op | source)
XLA Modules:
  0.0 67.9 jit_solution(2379887647871271594)
XLA Ops:
  0.6 64.5 %duct_step.1 = (f32[6,4,512]{2,1,0:T(4,128)}, f32[2,4,512]{2,1,0:T(4,128)}, f32[2,4,512]{2,1,0:T(4,128)}) custom-call(f32[6,4,512]{2,1,0:T(4,128)} %bitcast.11, f32[2,4,512]{2,1,0:T(4,128)} %bitcast.13, f32[140,8,128]{2,1,0:T(8,128)} %constant.2.clone.table_hbm), custom_call_target="tpu_custom_call" | custom-call | tf_op jit(solution)/shard_map/duct_step/pallas_call | solution.py:499
  65.1 0.0 copy-start.1
  65.1 1.4 %copy.12 = f32[3,2,1,4,512]{4,3,2,1,0:T(4,128)} copy(f32[3,2,1,4,512]{4,3,2,1,0:T(4,128)} %bitcast.12) | data formatting | bytes 98304
  66.6 0.0 copy-done.1
  66.6 0.0 copy-start
  66.6 0.6 copy.13
  67.2 0.1 copy-done
  67.3 0.6 copy.14
Async XLA Ops:
  65.1 1.4 %copy-start.1 = (f32[2,4,512]{2,1,0:T(4,128)S(1)}, f32[2,4,512]{2,1,0:T(4,128)}, u32[]{:S(2)}) copy-start(f32[2,4,512]{2,1,0:T(4,128)} %get-tuple-element.7) | copy-start | bytes 49156
  66.6 0.7 %copy-start = (f32[2,4,512]{2,1,0:T(4,128)S(1)}, f32[2,4,512]{2,1,0:T(4,128)}, u32[]{:S(2)}) copy-start(f32[2,4,512]{2,1,0:T(4,128)} %get-tuple-element.8) | copy-start | bytes 49156

commit v2 on v1

--- a/solution.py
+++ b/solution.py
@@ -10,7 +10,8 @@
 STEP = 0.02
 HALF = 64
 OFFSETS = ((-1, 0), (1, 0), (0, -1), (0, 1), (-1, -1), (1, -1), (-1, 1), (1, 1))
-ROUND_FIELDS = (4, 3, 3, 1, 1, 1, 1, 1)
+ROUND_FIELDS = (3, 3, 3, 2, 1, 1, 1, 1)
+GROUPS = ((0, 3), (3, 4), (7, 1), (8, 1))
 
 
 def roll(values, shift, axis):
@@ -111,12 +112,26 @@
 
     def group(self, stage, i):
         if stage == 0:
-            me = self.x * 2 + self.core
-            other = rem(me + i, 8)
-            return self.mesh_id(div(other, 2), self.y, self.z, rem(other, 2)), me
-        if stage == 1:
-            return self.mesh_id(self.x, rem(self.y + i, 8), self.z, self.core), self.y
-        return self.mesh_id(self.x, self.y, rem(self.z + i, 8), self.core), self.z
+            return self.mesh_id(self.x, self.y, rem(self.z + i // 2, 8), rem(self.core + i % 2, 2))
+        return self.mesh_id(rem(self.x + i // 8, 4), rem(self.y + i % 8, 8), self.z, self.core)
+
+
+MEMBERS = (16, 32)
+
+
+def far_first(stage):
+    def hops(i):
+        if stage == 0:
+            return (min(i // 2, 8 - i // 2), i % 2)
+        return (min(i // 8, 4 - i // 8) + min(i % 8, 8 - i % 8), 0)
+
+    return sorted(range(1, MEMBERS[stage]), key=hops, reverse=True)
+
+
+def mirror(stage, i):
+    if stage == 0:
+        return (8 - i // 2) % 8 * 2 + i % 2
+    return (4 - i // 8) % 4 * 8 + (8 - i % 8) % 8
 
 
 class Masks:
@@ -240,9 +255,13 @@
     return [ka[i] + wa[i] * (kb[i] + kc[i]) + scaled[i] * p[i] for i in range(4)]
 
 
-def moment(f, g, weight=None):
+def moment(k, f, g, weight=None):
     total = sum_of([f[i][0] * g[i][0] if weight is None else f[i][0] * g[i][0] * weight[i] for i in range(4)])
-    return jnp.sum(total, axis=0, keepdims=True)
+    total = jnp.sum(total, axis=0, keepdims=True)
+    for shift in (64, 32, 16):
+        total = total + roll(total, shift, 1)
+    lane = lax.broadcasted_iota(jnp.int32, (1, 128), 1)
+    return jnp.where((lane >> 4) == k, total, 0.0)
 
 
 def solve(n, e):
@@ -265,19 +284,18 @@
     return out
 
 
-def kernel(vel_hbm, react_hbm, table_hbm, velo_ref, press_ref, resid_ref, vel, react, tab, load_sem,
+def kernel(vel_hbm, react_hbm, table_hbm, home_ref, total_ref, vel, react, tab, load_sem,
            send0, recv0, sem0, *rest):
     rounds = len(ROUND_FIELDS)
     send_x, send_z = rest[0:rounds], rest[rounds:2 * rounds]
     got_refs = rest[2 * rounds:3 * rounds]
-    (round_sem, sums, part, sum_sem, back_send, back_recv, back_sem, scratch) = rest[3 * rounds:]
+    (round_sem, part, sums0, sums1, sum_sem, back_send, back_recv, back_sem) = rest[3 * rounds:]
+    sums = (sums0, sums1)
     place = Place(lax.axis_index("gx"), lax.axis_index("gy"), lax.axis_index("gz"))
 
-    def push(pairs, device, send_sem, recv_sem, own=None):
+    def push(source, target, device, send_sem, recv_sem, own=None):
         def remote():
-            for source, target in pairs:
-                pltpu.make_async_remote_copy(source, target, send_sem, recv_sem,
-                                             device_id=device, device_id_type=MESH).start()
+            pltpu.make_async_remote_copy(source, target, send_sem, recv_sem, device_id=device, device_id_type=MESH).start()
 
         if own is None:
             remote()
@@ -286,8 +304,7 @@
 
         @pl.when(own)
         def _():
-            for source, target in pairs:
-                pltpu.make_async_copy(source, target, recv_sem).start()
+            pltpu.make_async_copy(source, target, recv_sem).start()
 
     def greet(device):
         pl.semaphore_signal(barrier, inc=1, device_id=device, device_id_type=MESH)
@@ -301,9 +318,9 @@
     for dx, dz in OFFSETS:
         greet(place.neighbour(dx, dz))
         count += 1
-    for stage in range(3):
-        for i in range(1, 8):
-            greet(place.group(stage, i)[0])
+    for stage in range(2):
+        for i in far_first(stage):
+            greet(place.group(stage, i))
             count += 1
 
     loads = [pltpu.make_async_copy(s, d, load_sem.at[k]) for k, (s, d) in
@@ -318,15 +335,14 @@
             for i in range(4):
                 lanes = slice(i * 128, (i + 1) * 128)
                 piece = vel[2 * f + x, :, lanes] if f < 3 else react[x, :, lanes]
-                send0[pl.ds(f * 8 + x * 4 + i, 4, stride=32), :] = piece
+                send0.reshape(128, 128)[pl.ds(f * 8 + x * 4 + i, 4, stride=32), :] = piece
     pl.semaphore_wait(barrier, count)
 
     own = place.x == place.gy
     into = pl.ds(pl.multiple_of(place.gy * 8, 8), 8)
-    for i in range(4):
+    for i in (2, 1, 3, 0):
         device, turn = place.worker(i)
-        pairs = [(send0.at[pl.ds(pl.multiple_of(turn * 32 + f * 8, 8), 8)], recv0.at[f, into]) for f in range(4)]
-        push(pairs, device, sem0.at[i], sem0.at[4], None if i else own)
+        push(send0.at[turn], recv0.at[:, into], device, sem0.at[i], sem0.at[4], None if i else own)
 
     loads[2].wait()
 
@@ -341,7 +357,7 @@
         axial, depth = pack(v, m)
         send_x[r][...] = axial
         send_z[r][...] = depth
-        for k, (dx, dz) in enumerate(OFFSETS):
+        for dx, dz in OFFSETS[4:] + OFFSETS[:4]:
             slot = OFFSETS.index((-dx, -dz))
             pltpu.make_async_remote_copy(
                 send_x[r] if dz == 0 else send_z[r], got_refs[r].at[slot],
@@ -356,21 +372,15 @@
     def assemble(r, v):
         return finish(r, begin(r, v))
 
-    groups = ((0, 4), (4, 3), (7, 1), (8, 1))
-
     def give_back(g):
-        first, number = groups[g]
+        first, number = GROUPS[g]
+        fields = pl.ds(first, number)
         into = pl.ds(pl.multiple_of(place.turn * 8, 8), 8)
-        for i in range(4):
+        for i in (2, 1, 3, 0):
             device, cross = place.home(i)
             rows = pl.ds(pl.multiple_of(cross * 8, 8), 8)
-            pairs = [(back_send.at[f, rows], back_recv.at[f, into]) for f in range(first, first + number)]
-            push(pairs, device, back_sem.at[i, g], back_sem.at[4, g], None if i else own)
-
-    def returned(g):
-        first, number = groups[g]
-        ref = back_recv.at[pl.ds(first, number)]
-        pltpu.make_async_copy(ref, ref, back_sem.at[4, g]).wait()
+            push(back_send.at[fields, rows], back_recv.at[fields, into], device,
+                 back_sem.at[i, g], back_sem.at[4, g], None if i else own)
 
     def keep(f, v):
         for i in range(4):
@@ -379,95 +389,73 @@
     mass = constant(get, "mass")
     scaled = [fields[i][3:4] * mass[i] for i in range(4)]
     diag_local = constant(get, "diag")
-    v = [jnp.concatenate([fields[i][0:3], scaled[i] + diag_local[i]], axis=0) for i in range(4)]
-    v = assemble(0, v)
-    diag = [x[3:4] for x in v]
-    inverse_diag = [1.0 / x for x in diag]
-    u = [v[i][0:3] * m.inverse[i] for i in range(4)]
-    keep(3, [x[0] for x in diag])
+    v = assemble(0, [x[0:3] for x in fields])
+    u = [v[i] * m.inverse[i] for i in range(4)]
     tend = constant(get, "tend")
     tend = [tend[i] * m.inverse[i] * m.interior for i in range(4)]
     for r in (1, 2):
         t = assemble(r, transport(u, get, m))
         u = [m.interior * u[i] - tend[i] * t[i] for i in range(4)]
+    v = divergence(u, get, m)
+    v = begin(3, [jnp.concatenate([v[i], scaled[i] + diag_local[i]], axis=0) for i in range(4)])
     for k in range(3):
         keep(k, [x[k] for x in u])
-    source = begin(3, divergence(u, get, m))
     give_back(0)
-    source = finish(3, source)
+    v = finish(3, v)
+    source, diag = [x[0:1] for x in v], [x[1:2] for x in v]
+    inverse_diag = [1.0 / x for x in diag]
 
     q = [[source[i] * inverse_diag[i] for i in range(4)]]
     weight = [diag[i][0] * m.inverse[i] for i in range(4)]
-    part[0, 0:1, :] = moment(q[0], source, m.inverse)
-    keep(4, [x[0] for x in q[0]])
     for j in range(3):
         w = begin(4 + j, stiffness(q[j], scaled, get, m))
+        if j == 0:
+            sums_early = moment(0, q[0], source, m.inverse)
+            keep(3, [x[0] for x in diag])
         if j == 1:
-            part[0, 2:3, :] = moment(q[1], q[1], weight)
+            sums_early = sums_early + moment(1, q[0], q[1], weight) + moment(2, q[1], q[1], weight)
+        if j == 2:
+            sums_early = sums_early + moment(3, q[1], q[2], weight) + moment(4, q[2], q[2], weight)
+        keep(4 + j, [x[0] for x in q[j]])
         if j == 2:
             give_back(1)
-            part[0, 3:4, :] = moment(q[1], q[2], weight)
-            part[0, 4:5, :] = moment(q[2], q[2], weight)
-        if j == 1:
-            part[0, 1:2, :] = moment(q[0], q[1], weight)
         w = finish(4 + j, w)
         q.append([w[i] * inverse_diag[i] - q[j][i] for i in range(4)])
-        keep(5 + j, [x[0] for x in q[j + 1]])
     w = stiffness(q[3], scaled, get, m)
-    part[0, 5:6, :] = moment(q[2], q[3], weight)
-    part[0, 6:7, :] = moment(q[3], q[3], weight)
-    part[0, 7:8, :] = moment(q[3], w)
+    part[0] = (sums_early + moment(5, q[2], q[3], weight)) + (moment(6, q[3], q[3], weight) + moment(7, q[3], w))
 
     def send_sum(stage):
-        for i in range(1, 8):
-            device, me = place.group(stage, i)
-            pltpu.make_async_remote_copy(part.at[stage], sums.at[stage, 7 - i], sum_sem.at[0, stage],
-                                         sum_sem.at[1, stage], device_id=device, device_id_type=MESH).start()
+        for i in far_first(stage):
+            pltpu.make_async_remote_copy(part.at[stage], sums[stage].at[mirror(stage, i) - 1], sum_sem.at[0, stage],
+                                         sum_sem.at[1, stage], device_id=place.group(stage, i), device_id_type=MESH).start()
 
     def take_sum(stage):
-        pltpu.make_async_copy(sums.at[stage], sums.at[stage], sum_sem.at[1, stage]).wait()
-        return sum_of([part[stage]] + [sums[stage, i] for i in range(7)])
+        pltpu.make_async_copy(sums[stage], sums[stage], sum_sem.at[1, stage]).wait()
+        return sum_of([part[stage]] + [sums[stage][i] for i in range(MEMBERS[stage] - 1)])
 
     send_sum(0)
     w = begin(7, w)
+    keep(7, [x[0] for x in q[3]])
     give_back(2)
     part[1] = take_sum(0)
     send_sum(1)
     w = finish(7, w)
     keep(8, [x[0] for x in w])
     give_back(3)
-
-    returned(0)
-    for f in range(3):
-        for x in range(2):
-            for i in range(4):
-                velo_ref[2 * f + x, :, i * 128:(i + 1) * 128] = back_recv[f, pl.ds(x * 4 + i, 4, stride=8), :]
-
-    part[2] = take_sum(1)
-    send_sum(2)
-    total = take_sum(2)
-    n = jnp.broadcast_to(jnp.sum(total, axis=1, keepdims=True), (8, 128))
-    c = solve([n[i:i + 1, :] for i in range(7)], n[7:8, :])
-
-    for g in (1, 2, 3):
-        returned(g)
-    d, q0, q1, q2, q3, w3 = [back_recv[f] for f in range(3, 9)]
-    scratch[0] = c[0] * q0 + c[1] * q1 + c[2] * q2 + c[3] * q3
-    scratch[1] = d * (q0 - c[0] * (q0 + q1) - c[1] * (q1 + q2) - c[2] * (q2 + q3)) - c[3] * w3
-    for f, ref in ((0, press_ref), (1, resid_ref)):
-        for x in range(2):
-            for i in range(4):
-                ref[x, :, i * 128:(i + 1) * 128] = scratch[f, pl.ds(x * 4 + i, 4, stride=8), :]
+    for g, (first, number) in enumerate(GROUPS):
+        ref = back_recv.at[pl.ds(first, number)]
+        pltpu.make_async_copy(ref, ref, back_sem.at[4, g]).wait()
+    home_ref[...] = back_recv[...]
 
     for r in range(rounds):
         pltpu.make_async_copy(got_refs[r], got_refs[r], round_sem.at[0, r]).wait()
-    for stage in range(3):
-        pltpu.make_async_copy(sums.at[stage], sums.at[stage], sum_sem.at[0, stage]).wait()
+    for stage in range(2):
+        pltpu.make_async_copy(sums[stage], sums[stage], sum_sem.at[0, stage]).wait()
 
     def sent(i):
         ref = recv0.at[:, pl.ds(0, 8)]
         pltpu.make_async_copy(ref, ref, sem0.at[i]).wait()
-        for g, (first, number) in enumerate(groups):
+        for g, (first, number) in enumerate(GROUPS):
             ref = back_recv.at[pl.ds(first, number), pl.ds(0, 8)]
             pltpu.make_async_copy(ref, ref, back_sem.at[i, g]).wait()
 
@@ -477,6 +465,26 @@
     @pl.when(jnp.logical_not(own))
     def _():
         sent(0)
+
+    total_ref[...] = take_sum(1)
+
+
+def combine(home, total_ref, velo_ref, press_ref, resid_ref, scratch):
+    lane = lax.broadcasted_iota(jnp.int32, (8, 128), 1)
+    row = lax.broadcasted_iota(jnp.int32, (8, 128), 0)
+    n = jnp.sum(jnp.where((lane >> 4) == row, total_ref[...], 0.0), axis=1, keepdims=True)
+    n = jnp.broadcast_to(n, (8, 128))
+    c = solve([n[i:i + 1, :] for i in range(7)], n[7:8, :])
+    d, q0, q1, q2, q3, w3 = [home[f] for f in range(3, 9)]
+    scratch[0] = c[0] * q0 + c[1] * q1 + c[2] * q2 + c[3] * q3
+    scratch[1] = d * (q0 - c[0] * (q0 + q1) - c[1] * (q1 + q2) - c[2] * (q2 + q3)) - c[3] * w3
+    for x in range(2):
+        for i in range(4):
+            rows, lanes = pl.ds(x * 4 + i, 4, stride=8), slice(i * 128, (i + 1) * 128)
+            press_ref[x, :, lanes] = scratch[0, rows, :]
+            resid_ref[x, :, lanes] = scratch[1, rows, :]
+            for f in range(3):
+                velo_ref[2 * f + x, :, lanes] = home[f, rows, :]
 
 
 def body(velocity, reaction, table):
@@ -486,25 +494,33 @@
     scratch = [
         pltpu.VMEM((6, 4, 512), f32), pltpu.VMEM((2, 4, 512), f32), pltpu.VMEM(table.shape, f32),
         pltpu.SemaphoreType.DMA((3,)),
-        pltpu.VMEM((128, 128), f32), pltpu.VMEM((4, 32, 128), f32), pltpu.SemaphoreType.DMA((5,)),
+        pltpu.VMEM((4, 4, 8, 128), f32), pltpu.VMEM((4, 32, 128), f32), pltpu.SemaphoreType.DMA((5,)),
     ]
     scratch += [pltpu.VMEM((n, 8, 128), f32) for n in ROUND_FIELDS] * 2
     scratch += [pltpu.VMEM((8, n, 8, 128), f32) for n in ROUND_FIELDS]
     scratch += [
         pltpu.SemaphoreType.DMA((2, len(ROUND_FIELDS))),
-        pltpu.VMEM((3, 7, 8, 128), f32), pltpu.VMEM((3, 8, 128), f32), pltpu.SemaphoreType.DMA((2, 3)),
+        pltpu.VMEM((2, 1, 128), f32), pltpu.VMEM((MEMBERS[0] - 1, 1, 128), f32), pltpu.VMEM((MEMBERS[1] - 1, 1, 128), f32),
+        pltpu.SemaphoreType.DMA((2, 2)),
         pltpu.VMEM((9, 32, 128), f32), pltpu.VMEM((9, 32, 128), f32), pltpu.SemaphoreType.DMA((5, 4)),
-        pltpu.VMEM((2, 32, 128), f32),
     ]
-    velo, press, resid = pl.pallas_call(
+    home, total = pl.pallas_call(
         kernel,
-        out_shape=[jax.ShapeDtypeStruct((6, 4, 512), f32)] + [jax.ShapeDtypeStruct((2, 4, 512), f32)] * 2,
+        out_shape=[jax.ShapeDtypeStruct((9, 32, 128), f32), jax.ShapeDtypeStruct((1, 128), f32)],
         in_specs=[spec] * 3,
-        out_specs=[vmem] * 3,
+        out_specs=[vmem] * 2,
         scratch_shapes=scratch,
         compiler_params=pltpu.CompilerParams(collective_id=0, has_side_effects=True),
         name="duct_step",
     )(velocity.reshape(6, 4, 512), reaction.reshape(2, 4, 512), table)
+    velo, press, resid = pl.pallas_call(
+        combine,
+        out_shape=[jax.ShapeDtypeStruct((6, 4, 512), f32)] + [jax.ShapeDtypeStruct((2, 4, 512), f32)] * 2,
+        in_specs=[vmem] * 2,
+        out_specs=[vmem] * 3,
+        scratch_shapes=[pltpu.VMEM((2, 32, 128), f32)],
+        name="combine",
+    )(home, total)
     return velo.reshape(velocity.shape), press.reshape(reaction.shape), resid.reshape(reaction.shape)
 
 

time: 68.5 us -> 64.6 us (0.943)
  local copies, waits for them, and re-layouts: 2.76 us -> 0 us
  Pallas kernels: 64.5 us -> 63.8 us
    unnamed x7 -> x0, local copies, waits for them, and re-layouts: 2.76 us -> none
    pallas_call x1 -> x2, Pallas kernels: 64.5 us -> 63.8 us  [the longest x1 62.1 us: body(): pl.pallas_call(kernel, out_shape=[jax.ShapeDtypeStruct((9, 32, 128), f32)...]
where the time goes in v2:
time: 64.6 us; the launch traced here: 64.4 us
  Pallas kernels  63.8 us (99%)
    pallas_call x1, Pallas kernels, body(): pl.pallas_call(kernel, out_shape=[jax.ShapeDtypeStruct((9, 32, 128), f32)...  62.1 us
    pallas_call x1, Pallas kernels, body(): pl.pallas_call(combine, out_shape=[jax.ShapeDtypeStruct((6, 4, 512), f32)...  1.68 us

profile of v2, /device:TPU:1, one launch (start us, length us, event | category | flops | bytes accessed | tf_op | source)
XLA Modules:
  0.0 64.4 jit_solution(9798809304811543349)
XLA Ops:
  0.6 62.1 %duct_step.1 = (f32[9,32,128]{2,1,0:T(8,128)}, f32[1,128]{1,0:T(1,128)}) custom-call(f32[6,4,512]{2,1,0:T(4,128)} %bitcast.11, f32[2,4,512]{2,1,0:T(4,128)} %bitcast.12, f32[140,8,128]{2,1,0:T(8,128)} %constant.2.clone.table_hbm), custom_call_target="tpu_custom_call" | custom-call | tf_op jit(solution)/shard_map/duct_step/pallas_call | solution.py:507
  62.7 1.7 %combine.1 = (f32[6,4,512]{2,1,0:T(4,128)}, f32[2,4,512]{2,1,0:T(4,128)}, f32[2,4,512]{2,1,0:T(4,128)}) custom-call(f32[9,32,128]{2,1,0:T(8,128)} %get-tuple-element.8.home, f32[1,128]{1,0:T(1,128)} %get-tuple-element.9.total_ref), custom_call_target="tpu_custom_call" | custom-call | tf_op jit(solution)/shard_map/combine/pallas_call | solution.py:516

commit v3 on v2

--- a/solution.py
+++ b/solution.py
@@ -10,7 +10,7 @@
 STEP = 0.02
 HALF = 64
 OFFSETS = ((-1, 0), (1, 0), (0, -1), (0, 1), (-1, -1), (1, -1), (-1, 1), (1, 1))
-ROUND_FIELDS = (3, 3, 3, 2, 1, 1, 1, 1)
+ROUNDS = ((3, 8), (1, 8), (3, 4), (3, 4), (1, 4), (1, 4), (1, 4), (1, 4), (1, 4))
 GROUPS = ((0, 3), (3, 4), (7, 1), (8, 1))
 
 
@@ -64,15 +64,16 @@
     put("da", along_a(d, one))
     put("db", shifts(d, b, one))
     put("dc", shifts(d, c, one))
-    put("ka", along_a(k, w[b] * w[c]))
-    put("kb", shifts(k, b, w[c]))
-    put("kc", shifts(k, c, w[b]))
+    put("ka", along_a(k, one))
+    put("kb", shifts(k, b, one))
+    put("kc", shifts(k, c, one))
+    s = (w[:, None] * d * d).sum(0)
     put("wa", [w[2 * i + a_lo] for i in range(4)])
-    mass = [w[2 * i + a_lo] * w[b] * w[c] for i in range(4)]
-    put("mass", mass)
-    put("tend", [STEP / m for m in mass])
-    s = (w[:, None] * d * d).sum(0)
-    put("diag", [s[2 * i + a_lo] * w[b] * w[c] + w[2 * i + a_lo] * s[b] * w[c] + w[2 * i + a_lo] * w[b] * s[c] for i in range(4)])
+    put("wb", [w[b]])
+    put("wc", [w[c]])
+    put("sa", [s[2 * i + a_lo] for i in range(4)])
+    put("sb", [s[b]])
+    put("sc", [s[c]])
     table = np.stack(stack).astype(np.float32)
     return np.ascontiguousarray(np.broadcast_to(table[:, None, :], (len(stack), 8, 128))), rows
 
@@ -159,20 +160,45 @@
         down = (depth > 0).astype(jnp.float32)
         self.zmask = jnp.where(self.slot_low, up, down)
         one = jnp.ones((8, 128), jnp.float32)
-        iy = jnp.where(self.b0 | self.b7, 0.5, one)
-        iz = jnp.where(self.c0, 1.0 - 0.5 * down, jnp.where(self.c7, 1.0 - 0.5 * up, one))
-        iyz = iy * iz
-        self.inverse = [iyz * jnp.where(self.low, 0.5, one), iyz, iyz, iyz * jnp.where(self.low, one, 0.5)]
+        first, last = jnp.where(self.low, 0.5, one), jnp.where(self.low, one, 0.5)
+        self.hx = [first, one, one, last]
+        self.hy = jnp.where(self.b0 | self.b7, 0.5, one)
+        self.hz = jnp.where(self.c0, 1.0 - 0.5 * down, jnp.where(self.c7, 1.0 - 0.5 * up, one))
+        self.inverse = [x * (self.hy * self.hz) for x in self.hx]
         wall_y = ((b == 0) & (cross == 0)) | ((b == 7) & (cross == 3))
         self.interior = jnp.where(wall_y, 0.0, jnp.where(self.c0, down, jnp.where(self.c7, up, one)))
 
 
-def join_block(v, m):
+class Weights:
+    def __init__(self, get, m):
+        def row(name, i=0):
+            return get(ROWS[name][0] + i)
+
+        self.wa, self.wb, self.wc = [row("wa", i) for i in range(4)], row("wb"), row("wc")
+        two_x, two_y, two_z = [1.0 / h for h in m.hx], 1.0 / m.hy, 1.0 / m.hz
+        self.mx, self.my, self.mz = [x * t for x, t in zip(self.wa, two_x)], self.wb * two_y, self.wc * two_z
+        self.yz = self.my * self.mz
+        self.xz = [x * self.mz for x in self.mx]
+        self.xy = [x * self.my for x in self.mx]
+        self.all = [x * self.yz for x in self.mx]
+        self.mass = [x * (self.wb * self.wc) for x in self.wa]
+        self.diag = [
+            row("sa", i) * two_x[i] * self.yz + row("sb") * two_y * self.xz[i] + row("sc") * two_z * self.xy[i]
+            for i in range(4)
+        ]
+
+
+def join_cross(v, m):
     out = []
     for x in v:
         g = roll(roll(x, 2, 1), -56, 2)
         h = roll(roll(x, -2, 1), 56, 2)
         out.append(x + jnp.where(m.b0, g, jnp.where(m.b7, h, 0.0)))
+    return out
+
+
+def join_block(v, m):
+    out = join_cross(v, m)
     first = roll(roll(out[3], 1, 1), HALF, 2)
     last = roll(roll(out[0], -1, 1), HALF, 2)
     out[0] = out[0] + jnp.where(m.in0, first, 0.0)
@@ -181,13 +207,28 @@
 
 
 def pack(v, m):
-    axial = jnp.where(m.low, v[0], v[3])
+    return jnp.where(m.low, v[0], v[3]), pack_depth(v, m)
+
+
+def pack_depth(v, m):
     depth = v[0]
     for i in range(1, 4):
         depth = jnp.where(m.c == i, roll(v[i], i, 2), depth)
     for i in range(4):
         depth = jnp.where(m.c == 4 + i, roll(v[i], i - 3, 2), depth)
-    return axial, depth
+    return depth
+
+
+def pack_axial(v, m):
+    faces = roll(jnp.where(m.low, v[0], v[3]), HALF, 2)
+    return jnp.where(m.even, roll(faces, -1, 1), roll(faces, 1, 1))
+
+
+def partners(own, got, m):
+    across = jnp.where(m.in0 | m.in3, own, jnp.where(m.low, got[0], got[1]))
+    face = jnp.where(m.slot_low, got[3], got[2]) * m.zmask
+    depth = [jnp.where(m.c7, roll(face, 7 - i, 2), jnp.where(m.c0, roll(face, -4 - i, 2), 0.0)) for i in range(4)]
+    return {0: jnp.where(m.low, across, 0.0), 3: jnp.where(m.low, 0.0, across)}, depth
 
 
 def unpack(v, got, m):
@@ -225,34 +266,6 @@
     while len(terms) > 1:
         terms = [terms[i] + terms[i + 1] if i + 1 < len(terms) else terms[i] for i in range(0, len(terms), 2)]
     return terms[0]
-
-
-def constant(get, name):
-    return [get(ROWS[name][0] + i) for i in range(4)]
-
-
-def transport(u, get, m):
-    da = along_a(u, get, "da", m)
-    db = along_lanes(u, get, "db", 8)
-    dc = along_lanes(u, get, "dc", 1)
-    mass = constant(get, "mass")
-    return [mass[i] * (u[i][0:1] * da[i] + u[i][1:2] * db[i] + u[i][2:3] * dc[i]) for i in range(4)]
-
-
-def divergence(u, get, m):
-    da = along_a([x[0:1] for x in u], get, "da", m)
-    db = along_lanes([x[1:2] for x in u], get, "db", 8)
-    dc = along_lanes([x[2:3] for x in u], get, "dc", 1)
-    mass = constant(get, "mass")
-    return [-mass[i] * (da[i] + db[i] + dc[i]) for i in range(4)]
-
-
-def stiffness(p, scaled, get, m):
-    ka = along_a(p, get, "ka", m)
-    kb = along_lanes(p, get, "kb", 8)
-    kc = along_lanes(p, get, "kc", 1)
-    wa = constant(get, "wa")
-    return [ka[i] + wa[i] * (kb[i] + kc[i]) + scaled[i] * p[i] for i in range(4)]
 
 
 def moment(k, f, g, weight=None):
@@ -286,7 +299,7 @@
 
 def kernel(vel_hbm, react_hbm, table_hbm, home_ref, total_ref, vel, react, tab, load_sem,
            send0, recv0, sem0, *rest):
-    rounds = len(ROUND_FIELDS)
+    rounds = len(ROUNDS)
     send_x, send_z = rest[0:rounds], rest[rounds:2 * rounds]
     got_refs = rest[2 * rounds:3 * rounds]
     (round_sem, part, sums0, sums1, sum_sem, back_send, back_recv, back_sem) = rest[3 * rounds:]
@@ -352,25 +365,24 @@
     pltpu.make_async_copy(recv0, recv0, sem0.at[4]).wait()
     fields = [jnp.stack([recv0[f, pl.ds(i, 8, stride=4), :] for f in range(4)]) for i in range(4)]
 
-    def begin(r, v):
-        v = join_block(v, m)
-        axial, depth = pack(v, m)
+    def send(r, axial, depth):
         send_x[r][...] = axial
         send_z[r][...] = depth
-        for dx, dz in OFFSETS[4:] + OFFSETS[:4]:
+        for dx, dz in OFFSETS[4:ROUNDS[r][1]] + OFFSETS[2:4] + OFFSETS[0:2]:
             slot = OFFSETS.index((-dx, -dz))
             pltpu.make_async_remote_copy(
                 send_x[r] if dz == 0 else send_z[r], got_refs[r].at[slot],
                 round_sem.at[0, r], round_sem.at[1, r],
                 device_id=place.neighbour(dx, dz), device_id_type=MESH).start()
-        return v
-
-    def finish(r, v):
+
+    def receive(r):
         pltpu.make_async_copy(got_refs[r], got_refs[r], round_sem.at[1, r]).wait()
-        return unpack(v, [got_refs[r][k] for k in range(8)], m)
-
-    def assemble(r, v):
-        return finish(r, begin(r, v))
+        return [got_refs[r][k] for k in range(ROUNDS[r][1])]
+
+    def send_faces(r, along_axis, along_depth):
+        axial = pack_axial(along_axis, m)
+        send(r, axial, pack_depth(along_depth, m))
+        return axial
 
     def give_back(g):
         first, number = GROUPS[g]
@@ -386,43 +398,83 @@
         for i in range(4):
             back_send[f, pl.ds(i, 8, stride=4), :] = v[i]
 
-    mass = constant(get, "mass")
-    scaled = [fields[i][3:4] * mass[i] for i in range(4)]
-    diag_local = constant(get, "diag")
-    v = assemble(0, [x[0:3] for x in fields])
+    v = join_block([x[0:3] for x in fields], m)
+    send(0, *pack(v, m))
+    wt = Weights(get, m)
+    scaled = [fields[i][3:4] * wt.mass[i] for i in range(4)]
+    react_sum = join_block(scaled, m)
+    send(1, *pack(react_sum, m))
+    inside = STEP * m.interior
+    rate = ([inside * h for h in m.hx], inside * m.hy, inside * m.hz)
+    v = unpack(v, receive(0), m)
     u = [v[i] * m.inverse[i] for i in range(4)]
-    tend = constant(get, "tend")
-    tend = [tend[i] * m.inverse[i] * m.interior for i in range(4)]
-    for r in (1, 2):
-        t = assemble(r, transport(u, get, m))
-        u = [m.interior * u[i] - tend[i] * t[i] for i in range(4)]
-    v = divergence(u, get, m)
-    v = begin(3, [jnp.concatenate([v[i], scaled[i] + diag_local[i]], axis=0) for i in range(4)])
+
+    for r in (2, 3):
+        da = along_a(u, get, "da", m)
+        dc = along_lanes(u, get, "dc", 1)
+        axial = send_faces(r, da, dc)
+        db = join_cross(along_lanes(u, get, "db", 8), m)
+        first = [rate[0][i] * u[i][0:1] for i in range(4)]
+        third = [rate[2] * u[i][2:3] for i in range(4)]
+        base = [m.interior * u[i] - (first[i] * da[i] + rate[1] * u[i][1:2] * db[i] + third[i] * dc[i]) for i in range(4)]
+        if r == 3:
+            react_sum = unpack(react_sum, receive(1), m)
+            diag = [wt.diag[i] + react_sum[i] for i in range(4)]
+            inverse_diag = [1.0 / x for x in diag]
+            step_a = [wt.yz * x for x in inverse_diag]
+            step_b = [wt.xz[i] * inverse_diag[i] for i in range(4)]
+            step_c = [wt.xy[i] * inverse_diag[i] for i in range(4)]
+            step_0 = [react_sum[i] * inverse_diag[i] - 1.0 for i in range(4)]
+            weight = [diag[i][0] * m.inverse[i] for i in range(4)]
+            keep(3, [x[0] for x in diag])
+        across, depth = partners(axial, receive(r), m)
+        u = [base[i] - third[i] * depth[i] for i in range(4)]
+        for i in across:
+            u[i] = u[i] - first[i] * across[i]
+
+    da = along_a([x[0:1] for x in u], get, "da", m)
+    dc = along_lanes([x[2:3] for x in u], get, "dc", 1)
+    axial = send_faces(4, da, dc)
     for k in range(3):
         keep(k, [x[k] for x in u])
     give_back(0)
-    v = finish(3, v)
-    source, diag = [x[0:1] for x in v], [x[1:2] for x in v]
-    inverse_diag = [1.0 / x for x in diag]
+    db = join_cross(along_lanes([x[1:2] for x in u], get, "db", 8), m)
+    volume = [-x for x in wt.all]
+    base = [volume[i] * (m.hx[i] * da[i] + m.hy * db[i] + m.hz * dc[i]) for i in range(4)]
+    across, depth = partners(axial, receive(4), m)
+    source = [base[i] + volume[i] * m.hz * depth[i] for i in range(4)]
+    for i in across:
+        source[i] = source[i] + volume[i] * m.hx[i] * across[i]
 
     q = [[source[i] * inverse_diag[i] for i in range(4)]]
-    weight = [diag[i][0] * m.inverse[i] for i in range(4)]
-    for j in range(3):
-        w = begin(4 + j, stiffness(q[j], scaled, get, m))
+    for j in range(4):
+        ka = along_a(q[j], get, "ka", m)
+        kc = along_lanes(q[j], get, "kc", 1)
+        if j < 3:
+            axial = send_faces(5 + j, ka, kc)
+        kb = along_lanes(q[j], get, "kb", 8)
         if j == 0:
-            sums_early = moment(0, q[0], source, m.inverse)
-            keep(3, [x[0] for x in diag])
+            early = moment(0, q[0], source, m.inverse)
         if j == 1:
-            sums_early = sums_early + moment(1, q[0], q[1], weight) + moment(2, q[1], q[1], weight)
+            early = early + moment(1, q[0], q[1], weight) + moment(2, q[1], q[1], weight)
         if j == 2:
-            sums_early = sums_early + moment(3, q[1], q[2], weight) + moment(4, q[2], q[2], weight)
+            early = early + moment(3, q[1], q[2], weight) + moment(4, q[2], q[2], weight)
+        if j == 3:
+            break
+        kb = join_cross(kb, m)
+        base = [step_a[i] * ka[i] + step_b[i] * kb[i] + step_c[i] * kc[i] + step_0[i] * q[j][i] for i in range(4)]
         keep(4 + j, [x[0] for x in q[j]])
         if j == 2:
             give_back(1)
-        w = finish(4 + j, w)
-        q.append([w[i] * inverse_diag[i] - q[j][i] for i in range(4)])
-    w = stiffness(q[3], scaled, get, m)
-    part[0] = (sums_early + moment(5, q[2], q[3], weight)) + (moment(6, q[3], q[3], weight) + moment(7, q[3], w))
+        across, depth = partners(axial, receive(5 + j), m)
+        after = [base[i] + step_c[i] * depth[i] for i in range(4)]
+        for i in across:
+            after[i] = after[i] + step_a[i] * across[i]
+        q.append(after)
+    energy = [
+        wt.wb * wt.wc * ka[i] + wt.wa[i] * (wt.wc * kb[i] + wt.wb * kc[i]) + scaled[i] * q[3][i] for i in range(4)
+    ]
+    part[0] = (early + moment(5, q[2], q[3], weight)) + (moment(6, q[3], q[3], weight) + moment(7, q[3], energy))
 
     def send_sum(stage):
         for i in far_first(stage):
@@ -434,18 +486,24 @@
         return sum_of([part[stage]] + [sums[stage][i] for i in range(MEMBERS[stage] - 1)])
 
     send_sum(0)
-    w = begin(7, w)
+    axial = send_faces(8, ka, kc)
+    kb = join_cross(kb, m)
+    base = [wt.yz * ka[i] + wt.xz[i] * kb[i] + wt.xy[i] * kc[i] + react_sum[i] * q[3][i] for i in range(4)]
     keep(7, [x[0] for x in q[3]])
     give_back(2)
     part[1] = take_sum(0)
     send_sum(1)
-    w = finish(7, w)
+    across, depth = partners(axial, receive(8), m)
+    w = [base[i] + wt.xy[i] * depth[i] for i in range(4)]
+    for i in across:
+        w[i] = w[i] + wt.yz * across[i]
     keep(8, [x[0] for x in w])
     give_back(3)
     for g, (first, number) in enumerate(GROUPS):
         ref = back_recv.at[pl.ds(first, number)]
         pltpu.make_async_copy(ref, ref, back_sem.at[4, g]).wait()
-    home_ref[...] = back_recv[...]
+    leave = pltpu.make_async_copy(back_recv, home_ref, load_sem.at[0])
+    leave.start()
 
     for r in range(rounds):
         pltpu.make_async_copy(got_refs[r], got_refs[r], round_sem.at[0, r]).wait()
@@ -467,6 +525,7 @@
         sent(0)
 
     total_ref[...] = take_sum(1)
+    leave.wait()
 
 
 def combine(home, total_ref, velo_ref, press_ref, resid_ref, scratch):
@@ -496,10 +555,10 @@
         pltpu.SemaphoreType.DMA((3,)),
         pltpu.VMEM((4, 4, 8, 128), f32), pltpu.VMEM((4, 32, 128), f32), pltpu.SemaphoreType.DMA((5,)),
     ]
-    scratch += [pltpu.VMEM((n, 8, 128), f32) for n in ROUND_FIELDS] * 2
-    scratch += [pltpu.VMEM((8, n, 8, 128), f32) for n in ROUND_FIELDS]
+    scratch += [pltpu.VMEM((n, 8, 128), f32) for n, _ in ROUNDS] * 2
+    scratch += [pltpu.VMEM((k, n, 8, 128), f32) for n, k in ROUNDS]
     scratch += [
-        pltpu.SemaphoreType.DMA((2, len(ROUND_FIELDS))),
+        pltpu.SemaphoreType.DMA((2, len(ROUNDS))),
         pltpu.VMEM((2, 1, 128), f32), pltpu.VMEM((MEMBERS[0] - 1, 1, 128), f32), pltpu.VMEM((MEMBERS[1] - 1, 1, 128), f32),
         pltpu.SemaphoreType.DMA((2, 2)),
         pltpu.VMEM((9, 32, 128), f32), pltpu.VMEM((9, 32, 128), f32), pltpu.SemaphoreType.DMA((5, 4)),
@@ -508,7 +567,7 @@
         kernel,
         out_shape=[jax.ShapeDtypeStruct((9, 32, 128), f32), jax.ShapeDtypeStruct((1, 128), f32)],
         in_specs=[spec] * 3,
-        out_specs=[vmem] * 2,
+        out_specs=[spec, vmem],
         scratch_shapes=scratch,
         compiler_params=pltpu.CompilerParams(collective_id=0, has_side_effects=True),
         name="duct_step",

time: 64.6 us -> 58.8 us (0.910)
  Pallas kernels: 63.8 us -> 58 us
    pallas_call x1, Pallas kernels: 62.1 us -> 56.3 us  [body(): pl.pallas_call(kernel, out_shape=[jax.ShapeDtypeStruct((9, 32, 128), f32)...]
where the time goes in v3:
time: 58.8 us; the launch traced here: 58.6 us
  Pallas kernels  58 us (99%)
  between operations  0.64 us (1%)
    pallas_call x1, Pallas kernels, body(): pl.pallas_call(kernel, out_shape=[jax.ShapeDtypeStruct((9, 32, 128), f32)...  56.3 us
    pallas_call x1, Pallas kernels, body(): pl.pallas_call(combine, out_shape=[jax.ShapeDtypeStruct((6, 4, 512), f32)...  1.68 us

profile of v3, /device:TPU:1, one launch (start us, length us, event | category | flops | bytes accessed | tf_op | source)
XLA Modules:
  0.0 58.6 jit_solution(5669114114419260024)
XLA Ops:
  0.6 56.3 %duct_step.1 = (f32[9,32,128]{2,1,0:T(8,128)}, f32[1,128]{1,0:T(1,128)}) custom-call(f32[6,4,512]{2,1,0:T(4,128)} %bitcast.11, f32[2,4,512]{2,1,0:T(4,128)} %bitcast.12, f32[136,8,128]{2,1,0:T(8,128)} %constant.2.clone.table_hbm), custom_call_target="tpu_custom_call" | custom-call | tf_op jit(solution)/shard_map/duct_step/pallas_call | solution.py:566
  56.9 1.7 %combine.1 = (f32[6,4,512]{2,1,0:T(4,128)}, f32[2,4,512]{2,1,0:T(4,128)}, f32[2,4,512]{2,1,0:T(4,128)}) custom-call(f32[9,32,128]{2,1,0:T(8,128)} %get-tuple-element.8.home, f32[1,128]{1,0:T(1,128)} %get-tuple-element.9.total_ref), custom_call_target="tpu_custom_call" | custom-call | tf_op jit(solution)/shard_map/combine/pallas_call | solution.py:575

commit v4 on v3

--- a/solution.py
+++ b/solution.py
@@ -9,8 +9,8 @@
 MESH = pl.DeviceIdType.MESH
 STEP = 0.02
 HALF = 64
-OFFSETS = ((-1, 0), (1, 0), (0, -1), (0, 1), (-1, -1), (1, -1), (-1, 1), (1, 1))
-ROUNDS = ((3, 8), (1, 8), (3, 4), (3, 4), (1, 4), (1, 4), (1, 4), (1, 4), (1, 4))
+OFFSETS = ((-1, 0), (1, 0), (0, -1), (0, 1), (-1, -1), (1, -1), (-1, 1), (1, 1), (0, -2), (0, 2))
+ROUNDS = ((3, 8), (1, 8), (3, 4), (3, 4), (2, 10), (2, 10), (1, 4))
 GROUPS = ((0, 3), (3, 4), (7, 1), (8, 1))
 
 
@@ -75,10 +75,11 @@
     put("sb", [s[b]])
     put("sc", [s[c]])
     table = np.stack(stack).astype(np.float32)
-    return np.ascontiguousarray(np.broadcast_to(table[:, None, :], (len(stack), 8, 128))), rows
-
-
-TABLE, ROWS = tables()
+    whole = np.ascontiguousarray(np.broadcast_to(table[:, None, :], (len(stack), 8, 128)))
+    return whole, rows, float(k[0, 0]), float(k[0, 7])
+
+
+TABLE, ROWS, NEAR, FAR = tables()
 
 
 def owner_of(axial, depth):
@@ -159,6 +160,9 @@
         up = (depth < 31).astype(jnp.float32)
         down = (depth > 0).astype(jnp.float32)
         self.zmask = jnp.where(self.slot_low, up, down)
+        self.far = jnp.where(self.slot_low, (depth < 30).astype(jnp.float32), (depth > 1).astype(jnp.float32)) * FAR
+        self.faces = self.c0 | self.c7
+        self.zhas = jnp.where(self.c0, down, jnp.where(self.c7, up, 0.0))
         one = jnp.ones((8, 128), jnp.float32)
         first, last = jnp.where(self.low, 0.5, one), jnp.where(self.low, one, 0.5)
         self.hx = [first, one, one, last]
@@ -213,9 +217,11 @@
 def pack_depth(v, m):
     depth = v[0]
     for i in range(1, 4):
-        depth = jnp.where(m.c == i, roll(v[i], i, 2), depth)
+        if v[i] is not None:
+            depth = jnp.where(m.c == i, roll(v[i], i, 2), depth)
     for i in range(4):
-        depth = jnp.where(m.c == 4 + i, roll(v[i], i - 3, 2), depth)
+        if v[i] is not None:
+            depth = jnp.where(m.c == 4 + i, roll(v[i], i - 3, 2), depth)
     return depth
 
 
@@ -224,10 +230,62 @@
     return jnp.where(m.even, roll(faces, -1, 1), roll(faces, 1, 1))
 
 
+def spread(face, i, m):
+    return jnp.where(m.c7, roll(face, 7 - i, 2), jnp.where(m.c0, roll(face, -4 - i, 2), 0.0))
+
+
+def edges(got, m):
+    before = jnp.where(m.slot_low, got[6], got[4])
+    after = jnp.where(m.slot_low, got[7], got[5])
+    return (jnp.where(m.edge0, roll(roll(before, -1, 1), -67, 2), 0.0)
+            + jnp.where(m.edge3, roll(roll(after, 1, 1), 67, 2), 0.0)) * m.zmask
+
+
+def pair_pack(fa, fc, base, pa, pc, get, m):
+    axial = pack_axial(fa, m)
+    own = list(base)
+    own[0] = own[0] + pa[0] * jnp.where(m.in0, axial, 0.0)
+    own[3] = own[3] + pa[3] * jnp.where(m.in3, axial, 0.0)
+    ka = along_a(own, get, "ka", m, (0, 3))
+    kc = along_lanes(own, get, "kc", 1)
+    reach = [pc[i] * fc[i] for i in range(4)]
+    ea = along_a([jnp.where(m.faces, x, 0.0) for x in reach], get, "ka", m, (0, 3))
+    first, last = along_lanes([jnp.where(m.low, pa[0] * fa[0], 0.0), jnp.where(m.low, 0.0, pa[3] * fa[3])], get, "kc", 1)
+    return (jnp.concatenate([axial, pack_axial(ka, m)], axis=0),
+            jnp.concatenate([pack_depth(fc, m), pack_depth(kc, m)], axis=0),
+            jnp.concatenate([pack_depth(ea, m), pack_depth([first, None, None, last], m)], axis=0),
+            jnp.concatenate([pack_depth(reach, m), pack_depth(reach, m)], axis=0))
+
+
+def pair_unpack(axial, got, fa, fc, base, pa, pc, get, m):
+    across, depth = partners(axial, [g[0:1] for g in got], m)
+    x = [base[i] + pc[i] * depth[i] for i in range(4)]
+    for i in across:
+        x[i] = x[i] + pa[i] * across[i]
+    ga = edges([g[0:1] for g in got], m)
+    second = [g[1:2] for g in got]
+    face = jnp.where(m.slot_low, second[3], second[2]) * m.zmask + edges(second, m)
+    face = face + jnp.where(m.slot_low, got[9][0:1], got[8][0:1]) * m.far
+    depth = [spread(face, i, m) + NEAR * m.zhas * (pc[i] * fc[i]) for i in range(4)]
+    across = {0: jnp.where(m.out0, second[0] + NEAR * (pa[0] * fa[0]), 0.0) + spread(ga, 0, m),
+              3: jnp.where(m.out3, second[1] + NEAR * (pa[3] * fa[3]), 0.0) + spread(ga, 3, m)}
+    return x, across, depth
+
+
+def operate(x, across, depth, step, get, m):
+    ka = along_a(x, get, "ka", m)
+    kb = join_cross(along_lanes(x, get, "kb", 8), m)
+    kc = along_lanes(x, get, "kc", 1)
+    axial = pack_axial(ka, m)
+    across = {0: across[0] + jnp.where(m.in0, axial, 0.0), 3: across[3] + jnp.where(m.in3, axial, 0.0)}
+    out = [step[1][i] * kb[i] + step[2][i] * (kc[i] + depth[i]) + step[3][i] * x[i] for i in range(4)]
+    return [out[i] + step[0][i] * (ka[i] + across[i] if i in across else ka[i]) for i in range(4)]
+
+
 def partners(own, got, m):
     across = jnp.where(m.in0 | m.in3, own, jnp.where(m.low, got[0], got[1]))
     face = jnp.where(m.slot_low, got[3], got[2]) * m.zmask
-    depth = [jnp.where(m.c7, roll(face, 7 - i, 2), jnp.where(m.c0, roll(face, -4 - i, 2), 0.0)) for i in range(4)]
+    depth = [spread(face, i, m) for i in range(4)]
     return {0: jnp.where(m.low, across, 0.0), 3: jnp.where(m.low, 0.0, across)}, depth
 
 
@@ -247,14 +305,14 @@
     ]
 
 
-def along_a(v, get, name, m):
+def along_a(v, get, name, m, wanted=range(4)):
     parts = []
     for x in v:
         turned = roll(x, HALF, 2)
         parts.append(jnp.where(m.low, x, turned))
         parts.append(jnp.where(m.low, turned, x))
     start = ROWS[name][0]
-    return [sum_of([get(start + j * 8 + q) * parts[q] for q in range(8)]) for j in range(4)]
+    return [sum_of([get(start + j * 8 + q) * parts[q] for q in range(8)]) if j in wanted else None for j in range(4)]
 
 
 def along_lanes(v, get, name, stride):
@@ -302,7 +360,7 @@
     rounds = len(ROUNDS)
     send_x, send_z = rest[0:rounds], rest[rounds:2 * rounds]
     got_refs = rest[2 * rounds:3 * rounds]
-    (round_sem, part, sums0, sums1, sum_sem, back_send, back_recv, back_sem) = rest[3 * rounds:]
+    (send_far, round_sem, part, sums0, sums1, sum_sem, back_send, back_recv, back_sem) = rest[3 * rounds:]
     sums = (sums0, sums1)
     place = Place(lax.axis_index("gx"), lax.axis_index("gy"), lax.axis_index("gz"))
 
@@ -365,14 +423,19 @@
     pltpu.make_async_copy(recv0, recv0, sem0.at[4]).wait()
     fields = [jnp.stack([recv0[f, pl.ds(i, 8, stride=4), :] for f in range(4)]) for i in range(4)]
 
-    def send(r, axial, depth):
+    def send(r, axial, depth, edge=None, far=None):
         send_x[r][...] = axial
         send_z[r][...] = depth
+        if edge is not None:
+            send_far[r % 2, 0] = edge
+            send_far[r % 2, 1] = far
         for dx, dz in OFFSETS[4:ROUNDS[r][1]] + OFFSETS[2:4] + OFFSETS[0:2]:
             slot = OFFSETS.index((-dx, -dz))
+            source = send_x[r] if dz == 0 else send_z[r]
+            if edge is not None and abs(dx) + abs(dz) == 2:
+                source = send_far.at[r % 2, 0 if dx else 1]
             pltpu.make_async_remote_copy(
-                send_x[r] if dz == 0 else send_z[r], got_refs[r].at[slot],
-                round_sem.at[0, r], round_sem.at[1, r],
+                source, got_refs[r].at[slot], round_sem.at[0, r], round_sem.at[1, r],
                 device_id=place.neighbour(dx, dz), device_id_type=MESH).start()
 
     def receive(r):
@@ -421,10 +484,11 @@
             react_sum = unpack(react_sum, receive(1), m)
             diag = [wt.diag[i] + react_sum[i] for i in range(4)]
             inverse_diag = [1.0 / x for x in diag]
-            step_a = [wt.yz * x for x in inverse_diag]
-            step_b = [wt.xz[i] * inverse_diag[i] for i in range(4)]
-            step_c = [wt.xy[i] * inverse_diag[i] for i in range(4)]
-            step_0 = [react_sum[i] * inverse_diag[i] - 1.0 for i in range(4)]
+            step = ([wt.yz * x for x in inverse_diag],
+                    [wt.xz[i] * inverse_diag[i] for i in range(4)],
+                    [wt.xy[i] * inverse_diag[i] for i in range(4)],
+                    [react_sum[i] * inverse_diag[i] - 1.0 for i in range(4)])
+            volume = [-wt.all[i] * inverse_diag[i] for i in range(4)]
             weight = [diag[i][0] * m.inverse[i] for i in range(4)]
             keep(3, [x[0] for x in diag])
         across, depth = partners(axial, receive(r), m)
@@ -434,43 +498,30 @@
 
     da = along_a([x[0:1] for x in u], get, "da", m)
     dc = along_lanes([x[2:3] for x in u], get, "dc", 1)
-    axial = send_faces(4, da, dc)
+    db = join_cross(along_lanes([x[1:2] for x in u], get, "db", 8), m)
+    base = [volume[i] * (m.hx[i] * da[i] + m.hy * db[i] + m.hz * dc[i]) for i in range(4)]
+    pa, pc = [volume[i] * m.hx[i] for i in range(4)], [volume[i] * m.hz for i in range(4)]
+    tiles = pair_pack(da, dc, base, pa, pc, get, m)
+    send(4, *tiles)
     for k in range(3):
         keep(k, [x[k] for x in u])
     give_back(0)
-    db = join_cross(along_lanes([x[1:2] for x in u], get, "db", 8), m)
-    volume = [-x for x in wt.all]
-    base = [volume[i] * (m.hx[i] * da[i] + m.hy * db[i] + m.hz * dc[i]) for i in range(4)]
-    across, depth = partners(axial, receive(4), m)
-    source = [base[i] + volume[i] * m.hz * depth[i] for i in range(4)]
-    for i in across:
-        source[i] = source[i] + volume[i] * m.hx[i] * across[i]
-
-    q = [[source[i] * inverse_diag[i] for i in range(4)]]
-    for j in range(4):
-        ka = along_a(q[j], get, "ka", m)
-        kc = along_lanes(q[j], get, "kc", 1)
-        if j < 3:
-            axial = send_faces(5 + j, ka, kc)
-        kb = along_lanes(q[j], get, "kb", 8)
-        if j == 0:
-            early = moment(0, q[0], source, m.inverse)
-        if j == 1:
-            early = early + moment(1, q[0], q[1], weight) + moment(2, q[1], q[1], weight)
-        if j == 2:
-            early = early + moment(3, q[1], q[2], weight) + moment(4, q[2], q[2], weight)
-        if j == 3:
-            break
-        kb = join_cross(kb, m)
-        base = [step_a[i] * ka[i] + step_b[i] * kb[i] + step_c[i] * kc[i] + step_0[i] * q[j][i] for i in range(4)]
+    x, across, depth = pair_unpack(tiles[0][0:1], receive(4), da, dc, base, pa, pc, get, m)
+    q = [x, operate(x, across, depth, step, get, m)]
+
+    ka, kb, kc = along_a(q[1], get, "ka", m), along_lanes(q[1], get, "kb", 8), along_lanes(q[1], get, "kc", 1)
+    kb = join_cross(kb, m)
+    base = [step[0][i] * ka[i] + step[1][i] * kb[i] + step[2][i] * kc[i] + step[3][i] * q[1][i] for i in range(4)]
+    tiles = pair_pack(ka, kc, base, step[0], step[2], get, m)
+    send(5, *tiles)
+    early = moment(0, q[0], q[0], weight) + moment(1, q[0], q[1], weight) + moment(2, q[1], q[1], weight)
+    for j in range(2):
         keep(4 + j, [x[0] for x in q[j]])
-        if j == 2:
-            give_back(1)
-        across, depth = partners(axial, receive(5 + j), m)
-        after = [base[i] + step_c[i] * depth[i] for i in range(4)]
-        for i in across:
-            after[i] = after[i] + step_a[i] * across[i]
-        q.append(after)
+    x, across, depth = pair_unpack(tiles[0][0:1], receive(5), ka, kc, base, step[0], step[2], get, m)
+    q += [x, operate(x, across, depth, step, get, m)]
+
+    early = early + moment(3, q[1], q[2], weight) + moment(4, q[2], q[2], weight)
+    ka, kb, kc = along_a(q[3], get, "ka", m), along_lanes(q[3], get, "kb", 8), along_lanes(q[3], get, "kc", 1)
     energy = [
         wt.wb * wt.wc * ka[i] + wt.wa[i] * (wt.wc * kb[i] + wt.wb * kc[i]) + scaled[i] * q[3][i] for i in range(4)
     ]
@@ -486,14 +537,16 @@
         return sum_of([part[stage]] + [sums[stage][i] for i in range(MEMBERS[stage] - 1)])
 
     send_sum(0)
-    axial = send_faces(8, ka, kc)
+    axial = send_faces(6, ka, kc)
     kb = join_cross(kb, m)
     base = [wt.yz * ka[i] + wt.xz[i] * kb[i] + wt.xy[i] * kc[i] + react_sum[i] * q[3][i] for i in range(4)]
-    keep(7, [x[0] for x in q[3]])
+    for j in (2, 3):
+        keep(4 + j, [x[0] for x in q[j]])
+    give_back(1)
     give_back(2)
     part[1] = take_sum(0)
     send_sum(1)
-    across, depth = partners(axial, receive(8), m)
+    across, depth = partners(axial, receive(6), m)
     w = [base[i] + wt.xy[i] * depth[i] for i in range(4)]
     for i in across:
         w[i] = w[i] + wt.yz * across[i]
@@ -558,7 +611,7 @@
     scratch += [pltpu.VMEM((n, 8, 128), f32) for n, _ in ROUNDS] * 2
     scratch += [pltpu.VMEM((k, n, 8, 128), f32) for n, k in ROUNDS]
     scratch += [
-        pltpu.SemaphoreType.DMA((2, len(ROUNDS))),
+        pltpu.VMEM((2, 2, 2, 8, 128), f32), pltpu.SemaphoreType.DMA((2, len(ROUNDS))),
         pltpu.VMEM((2, 1, 128), f32), pltpu.VMEM((MEMBERS[0] - 1, 1, 128), f32), pltpu.VMEM((MEMBERS[1] - 1, 1, 128), f32),
         pltpu.SemaphoreType.DMA((2, 2)),
         pltpu.VMEM((9, 32, 128), f32), pltpu.VMEM((9, 32, 128), f32), pltpu.SemaphoreType.DMA((5, 4)),

time: 58.8 us -> 54.4 us (0.925)
  Pallas kernels: 58 us -> 53.6 us
    pallas_call x1, Pallas kernels: 56.3 us -> 51.9 us  [body(): pl.pallas_call(kernel, out_shape=[jax.ShapeDtypeStruct((9, 32, 128), f32)...]
where the time goes in v4:
time: 54.4 us; the launch traced here: 54.3 us
  Pallas kernels  53.6 us (99%)
  between operations  0.64 us (1%)
    pallas_call x1, Pallas kernels, body(): pl.pallas_call(kernel, out_shape=[jax.ShapeDtypeStruct((9, 32, 128), f32)...  51.9 us
    pallas_call x1, Pallas kernels, body(): pl.pallas_call(combine, out_shape=[jax.ShapeDtypeStruct((6, 4, 512), f32)...  1.68 us

profile of v4, /device:TPU:1, one launch (start us, length us, event | category | flops | bytes accessed | tf_op | source)
XLA Modules:
  0.0 54.3 jit_solution(15060847796116395228)
XLA Ops:
  0.6 51.9 %duct_step.1 = (f32[9,32,128]{2,1,0:T(8,128)}, f32[1,128]{1,0:T(1,128)}) custom-call(f32[6,4,512]{2,1,0:T(4,128)} %bitcast.11, f32[2,4,512]{2,1,0:T(4,128)} %bitcast.12, f32[136,8,128]{2,1,0:T(8,128)} %constant.2.clone.table_hbm), custom_call_target="tpu_custom_call" | custom-call | tf_op jit(solution)/shard_map/duct_step/pallas_call | solution.py:619
  52.6 1.7 %combine.1 = (f32[6,4,512]{2,1,0:T(4,128)}, f32[2,4,512]{2,1,0:T(4,128)}, f32[2,4,512]{2,1,0:T(4,128)}) custom-call(f32[9,32,128]{2,1,0:T(8,128)} %get-tuple-element.8.home, f32[1,128]{1,0:T(1,128)} %get-tuple-element.9.total_ref), custom_call_target="tpu_custom_call" | custom-call | tf_op jit(solution)/shard_map/combine/pallas_call | solution.py:628

commit v5 on v4

--- a/solution.py
+++ b/solution.py
@@ -386,6 +386,10 @@
         greet(place.worker(i)[0])
         greet(place.home(i)[0])
         count += 2
+    loads = [pltpu.make_async_copy(s, d, load_sem.at[k]) for k, (s, d) in
+             enumerate(((vel_hbm, vel), (react_hbm, react), (table_hbm, tab)))]
+    for copy in loads:
+        copy.start()
     for dx, dz in OFFSETS:
         greet(place.neighbour(dx, dz))
         count += 1
@@ -394,10 +398,6 @@
             greet(place.group(stage, i))
             count += 1
 
-    loads = [pltpu.make_async_copy(s, d, load_sem.at[k]) for k, (s, d) in
-             enumerate(((vel_hbm, vel), (react_hbm, react), (table_hbm, tab)))]
-    for copy in loads:
-        copy.start()
     m = Masks(place.depth)
     loads[0].wait()
     loads[1].wait()
@@ -411,17 +411,22 @@
 
     own = place.x == place.gy
     into = pl.ds(pl.multiple_of(place.gy * 8, 8), 8)
-    for i in (2, 1, 3, 0):
-        device, turn = place.worker(i)
-        push(send0.at[turn], recv0.at[:, into], device, sem0.at[i], sem0.at[4], None if i else own)
+    for part_of, fields in ((0, pl.ds(0, 3)), (1, pl.ds(3, 1))):
+        for i in (2, 1, 3, 0):
+            device, turn = place.worker(i)
+            push(send0.at[turn, fields], recv0.at[fields, into], device,
+                 sem0.at[part_of, i], sem0.at[part_of, 4], None if i else own)
 
     loads[2].wait()
 
     def get(row):
         return tab[row]
 
-    pltpu.make_async_copy(recv0, recv0, sem0.at[4]).wait()
-    fields = [jnp.stack([recv0[f, pl.ds(i, 8, stride=4), :] for f in range(4)]) for i in range(4)]
+    def taken(first, number):
+        ref = recv0.at[pl.ds(first, number)]
+        pltpu.make_async_copy(ref, ref, sem0.at[0 if number == 3 else 1, 4]).wait()
+        return [jnp.stack([recv0[f, pl.ds(i, 8, stride=4), :] for f in range(first, first + number)]) for i in range(4)]
+
 
     def send(r, axial, depth, edge=None, far=None):
         send_x[r][...] = axial
@@ -461,10 +466,10 @@
         for i in range(4):
             back_send[f, pl.ds(i, 8, stride=4), :] = v[i]
 
-    v = join_block([x[0:3] for x in fields], m)
+    v = join_block(taken(0, 3), m)
     send(0, *pack(v, m))
     wt = Weights(get, m)
-    scaled = [fields[i][3:4] * wt.mass[i] for i in range(4)]
+    scaled = [x * mass for x, mass in zip(taken(3, 1), wt.mass)]
     react_sum = join_block(scaled, m)
     send(1, *pack(react_sum, m))
     inside = STEP * m.interior
@@ -555,8 +560,7 @@
     for g, (first, number) in enumerate(GROUPS):
         ref = back_recv.at[pl.ds(first, number)]
         pltpu.make_async_copy(ref, ref, back_sem.at[4, g]).wait()
-    leave = pltpu.make_async_copy(back_recv, home_ref, load_sem.at[0])
-    leave.start()
+    home_ref[...] = back_recv[...]
 
     for r in range(rounds):
         pltpu.make_async_copy(got_refs[r], got_refs[r], round_sem.at[0, r]).wait()
@@ -564,8 +568,9 @@
         pltpu.make_async_copy(sums[stage], sums[stage], sum_sem.at[0, stage]).wait()
 
     def sent(i):
-        ref = recv0.at[:, pl.ds(0, 8)]
-        pltpu.make_async_copy(ref, ref, sem0.at[i]).wait()
+        for part_of, number in ((0, 3), (1, 1)):
+            ref = recv0.at[pl.ds(0, number), pl.ds(0, 8)]
+            pltpu.make_async_copy(ref, ref, sem0.at[part_of, i]).wait()
         for g, (first, number) in enumerate(GROUPS):
             ref = back_recv.at[pl.ds(first, number), pl.ds(0, 8)]
             pltpu.make_async_copy(ref, ref, back_sem.at[i, g]).wait()
@@ -578,7 +583,6 @@
         sent(0)
 
     total_ref[...] = take_sum(1)
-    leave.wait()
 
 
 def combine(home, total_ref, velo_ref, press_ref, resid_ref, scratch):
@@ -606,7 +610,7 @@
     scratch = [
         pltpu.VMEM((6, 4, 512), f32), pltpu.VMEM((2, 4, 512), f32), pltpu.VMEM(table.shape, f32),
         pltpu.SemaphoreType.DMA((3,)),
-        pltpu.VMEM((4, 4, 8, 128), f32), pltpu.VMEM((4, 32, 128), f32), pltpu.SemaphoreType.DMA((5,)),
+        pltpu.VMEM((4, 4, 8, 128), f32), pltpu.VMEM((4, 32, 128), f32), pltpu.SemaphoreType.DMA((2, 5)),
     ]
     scratch += [pltpu.VMEM((n, 8, 128), f32) for n, _ in ROUNDS] * 2
     scratch += [pltpu.VMEM((k, n, 8, 128), f32) for n, k in ROUNDS]
@@ -618,9 +622,9 @@
     ]
     home, total = pl.pallas_call(
         kernel,
-        out_shape=[jax.ShapeDtypeStruct((9, 32, 128), f32), jax.ShapeDtypeStruct((1, 128), f32)],
+        out_shape=[pltpu.VMEM((9, 32, 128), f32), pltpu.VMEM((1, 128), f32)],
         in_specs=[spec] * 3,
-        out_specs=[spec, vmem],
+        out_specs=[vmem] * 2,
         scratch_shapes=scratch,
         compiler_params=pltpu.CompilerParams(collective_id=0, has_side_effects=True),
         name="duct_step",
@@ -632,7 +636,7 @@
         out_specs=[vmem] * 3,
         scratch_shapes=[pltpu.VMEM((2, 32, 128), f32)],
         name="combine",
-    )(home, total)
+    )(pltpu.with_memory_space_constraint(home, pltpu.VMEM), pltpu.with_memory_space_constraint(total, pltpu.VMEM))
     return velo.reshape(velocity.shape), press.reshape(reaction.shape), resid.reshape(reaction.shape)
 
 

time: 54.4 us -> 52.8 us (0.971)
  Pallas kernels: 53.6 us -> 52 us
    pallas_call x1, Pallas kernels: 1.68 us -> 0.77 us  [body(): pl.pallas_call(combine, out_shape=[jax.ShapeDtypeStruct((6, 4, 512), f32)...]
    pallas_call x1, Pallas kernels: 51.9 us -> 51.3 us  [body(): pl.pallas_call(kernel, out_shape=[pltpu.VMEM((9, 32, 128), f32), pltpu.VM...]
where the time goes in v5:
time: 52.8 us; the launch traced here: 52.7 us
  Pallas kernels  52 us (98%)
  between operations  0.64 us (1%)
    pallas_call x1, Pallas kernels, body(): pl.pallas_call(kernel, out_shape=[pltpu.VMEM((9, 32, 128), f32), pltpu.VM...  51.3 us

profile of v5, /device:TPU:1, one launch (start us, length us, event | category | flops | bytes accessed | tf_op | source)
XLA Modules:
  0.0 52.7 jit_solution(14237855861502706016)
XLA Ops:
  0.6 51.3 %duct_step.1 = (f32[9,32,128]{2,1,0:T(8,128)S(1)}, f32[1,128]{1,0:T(1,128)S(1)}) custom-call(f32[6,4,512]{2,1,0:T(4,128)} %bitcast.11, f32[2,4,512]{2,1,0:T(4,128)} %bitcast.12, f32[136,8,128]{2,1,0:T(8,128)} %constant.2.clone.table_hbm), custom_call_target="tpu_custom_call" | custom-call | tf_op jit(solution)/shard_map/duct_step/pallas_call | solution.py:623
  51.9 0.8 %combine.1 = (f32[6,4,512]{2,1,0:T(4,128)}, f32[2,4,512]{2,1,0:T(4,128)}, f32[2,4,512]{2,1,0:T(4,128)}) custom-call(f32[9,32,128]{2,1,0:T(8,128)S(1)} %get-tuple-element.8.home, f32[1,128]{1,0:T(1,128)S(1)} %get-tuple-element.9.total_ref), custom_call_target="tpu_custom_call" | custom-call | tf_op jit(solution)/shard_map/combine/pallas_call | solution.py:632

commit v6 on v5

--- a/solution.py
+++ b/solution.py
@@ -225,6 +225,14 @@
     return depth
 
 
+def pack_edges(depth, m):
+    out = depth[0:1]
+    for k in range(1, depth.shape[0]):
+        moved = jnp.where(m.even, roll(depth[k:k + 1], k, 2), roll(depth[k:k + 1], -k, 2))
+        out = jnp.where((m.c & 3) == jnp.where(m.even, k, 3 - k), moved, out)
+    return out
+
+
 def pack_axial(v, m):
     faces = roll(jnp.where(m.low, v[0], v[3]), HALF, 2)
     return jnp.where(m.even, roll(faces, -1, 1), roll(faces, 1, 1))
@@ -294,10 +302,11 @@
     v[0] = v[0] + jnp.where(m.out0, roll(roll(got[0], -1, 1), HALF, 2), 0.0)
     v[3] = v[3] + jnp.where(m.out3, roll(roll(got[1], 1, 1), HALF, 2), 0.0)
     centre = jnp.where(m.slot_low, got[3], got[2])
-    before = jnp.where(m.slot_low, got[6], got[4])
-    after = jnp.where(m.slot_low, got[7], got[5])
-    face = centre + jnp.where(m.edge0, roll(roll(before, -1, 1), -67, 2), 0.0)
-    face = face + jnp.where(m.edge3, roll(roll(after, 1, 1), 67, 2), 0.0)
+    before = roll(jnp.where(m.slot_low, got[6], got[4]), -1, 1)
+    after = roll(jnp.where(m.slot_low, got[7], got[5]), 1, 1)
+    fields = range(v[0].shape[0])
+    face = centre + jnp.where(m.edge0, jnp.concatenate([roll(before, k - 67, 2) for k in fields], axis=0), 0.0)
+    face = face + jnp.where(m.edge3, jnp.concatenate([roll(after, 67 - k, 2) for k in fields], axis=0), 0.0)
     face = face * m.zmask
     return [
         v[i] + jnp.where(m.c7, roll(face, 7 - i, 2), jnp.where(m.c0, roll(face, -4 - i, 2), 0.0))
@@ -360,7 +369,7 @@
     rounds = len(ROUNDS)
     send_x, send_z = rest[0:rounds], rest[rounds:2 * rounds]
     got_refs = rest[2 * rounds:3 * rounds]
-    (send_far, round_sem, part, sums0, sums1, sum_sem, back_send, back_recv, back_sem) = rest[3 * rounds:]
+    (send_edge, send_far, round_sem, part, sums0, sums1, sum_sem, back_send, back_recv, back_sem) = rest[3 * rounds:]
     sums = (sums0, sums1)
     place = Place(lax.axis_index("gx"), lax.axis_index("gy"), lax.axis_index("gz"))
 
@@ -437,14 +446,20 @@
         for dx, dz in OFFSETS[4:ROUNDS[r][1]] + OFFSETS[2:4] + OFFSETS[0:2]:
             slot = OFFSETS.index((-dx, -dz))
             source = send_x[r] if dz == 0 else send_z[r]
+            target = got_refs[r].at[slot]
             if edge is not None and abs(dx) + abs(dz) == 2:
                 source = send_far.at[r % 2, 0 if dx else 1]
+            if r == 0:
+                target = got_refs[0].at[pl.ds(3 * slot, 3) if slot < 4 else pl.ds(8 + slot, 1)]
+                source = source if slot < 4 else send_edge
             pltpu.make_async_remote_copy(
-                source, got_refs[r].at[slot], round_sem.at[0, r], round_sem.at[1, r],
+                source, target, round_sem.at[0, r], round_sem.at[1, r],
                 device_id=place.neighbour(dx, dz), device_id_type=MESH).start()
 
     def receive(r):
         pltpu.make_async_copy(got_refs[r], got_refs[r], round_sem.at[1, r]).wait()
+        if r == 0:
+            return [got_refs[0][3 * k:3 * k + 3] if k < 4 else got_refs[0][8 + k:9 + k] for k in range(8)]
         return [got_refs[r][k] for k in range(ROUNDS[r][1])]
 
     def send_faces(r, along_axis, along_depth):
@@ -467,7 +482,9 @@
             back_send[f, pl.ds(i, 8, stride=4), :] = v[i]
 
     v = join_block(taken(0, 3), m)
-    send(0, *pack(v, m))
+    axial, depth = pack(v, m)
+    send_edge[...] = pack_edges(depth, m)
+    send(0, axial, depth)
     wt = Weights(get, m)
     scaled = [x * mass for x, mass in zip(taken(3, 1), wt.mass)]
     react_sum = join_block(scaled, m)
@@ -613,9 +630,9 @@
         pltpu.VMEM((4, 4, 8, 128), f32), pltpu.VMEM((4, 32, 128), f32), pltpu.SemaphoreType.DMA((2, 5)),
     ]
     scratch += [pltpu.VMEM((n, 8, 128), f32) for n, _ in ROUNDS] * 2
-    scratch += [pltpu.VMEM((k, n, 8, 128), f32) for n, k in ROUNDS]
+    scratch += [pltpu.VMEM((k, n, 8, 128) if r else (16, 8, 128), f32) for r, (n, k) in enumerate(ROUNDS)]
     scratch += [
-        pltpu.VMEM((2, 2, 2, 8, 128), f32), pltpu.SemaphoreType.DMA((2, len(ROUNDS))),
+        pltpu.VMEM((1, 8, 128), f32), pltpu.VMEM((2, 2, 2, 8, 128), f32), pltpu.SemaphoreType.DMA((2, len(ROUNDS))),
         pltpu.VMEM((2, 1, 128), f32), pltpu.VMEM((MEMBERS[0] - 1, 1, 128), f32), pltpu.VMEM((MEMBERS[1] - 1, 1, 128), f32),
         pltpu.SemaphoreType.DMA((2, 2)),
         pltpu.VMEM((9, 32, 128), f32), pltpu.VMEM((9, 32, 128), f32), pltpu.SemaphoreType.DMA((5, 4)),

time: 52.8 us -> 52.7 us (level)
  no operation moved by 1% of the time
where the time goes in v6:
time: 52.7 us; the launch traced here: 52.6 us
  Pallas kernels  52 us (99%)
  between operations  0.64 us (1%)
    pallas_call x1, Pallas kernels, body(): pl.pallas_call(kernel, out_shape=[pltpu.VMEM((9, 32, 128), f32), pltpu.VM...  51.2 us

profile of v6, /device:TPU:1, one launch (start us, length us, event | category | flops | bytes accessed | tf_op | source)
XLA Modules:
  0.0 52.6 jit_solution(16269616826710382040)
XLA Ops:
  0.6 51.2 %duct_step.1 = (f32[9,32,128]{2,1,0:T(8,128)S(1)}, f32[1,128]{1,0:T(1,128)S(1)}) custom-call(f32[6,4,512]{2,1,0:T(4,128)} %bitcast.11, f32[2,4,512]{2,1,0:T(4,128)} %bitcast.12, f32[136,8,128]{2,1,0:T(8,128)} %constant.2.clone.table_hbm), custom_call_target="tpu_custom_call" | custom-call | tf_op jit(solution)/shard_map/duct_step/pallas_call | solution.py:640
  51.8 0.8 %combine.1 = (f32[6,4,512]{2,1,0:T(4,128)}, f32[2,4,512]{2,1,0:T(4,128)}, f32[2,4,512]{2,1,0:T(4,128)}) custom-call(f32[9,32,128]{2,1,0:T(8,128)S(1)} %get-tuple-element.8.home, f32[1,128]{1,0:T(1,128)S(1)} %get-tuple-element.9.total_ref), custom_call_target="tpu_custom_call" | custom-call | tf_op jit(solution)/shard_map/combine/pallas_call | solution.py:649

commit v7 on v6

--- a/solution.py
+++ b/solution.py
@@ -242,11 +242,10 @@
     return jnp.where(m.c7, roll(face, 7 - i, 2), jnp.where(m.c0, roll(face, -4 - i, 2), 0.0))
 
 
-def edges(got, m):
-    before = jnp.where(m.slot_low, got[6], got[4])
-    after = jnp.where(m.slot_low, got[7], got[5])
-    return (jnp.where(m.edge0, roll(roll(before, -1, 1), -67, 2), 0.0)
-            + jnp.where(m.edge3, roll(roll(after, 1, 1), 67, 2), 0.0)) * m.zmask
+def edges(got, m, k):
+    before = roll(jnp.where(m.slot_low, got[6], got[4]), -1, 1)
+    after = roll(jnp.where(m.slot_low, got[7], got[5]), 1, 1)
+    return (jnp.where(m.edge0, roll(before, k - 67, 2), 0.0) + jnp.where(m.edge3, roll(after, 67 - k, 2), 0.0)) * m.zmask
 
 
 def pair_pack(fa, fc, base, pa, pc, get, m):
@@ -261,18 +260,18 @@
     first, last = along_lanes([jnp.where(m.low, pa[0] * fa[0], 0.0), jnp.where(m.low, 0.0, pa[3] * fa[3])], get, "kc", 1)
     return (jnp.concatenate([axial, pack_axial(ka, m)], axis=0),
             jnp.concatenate([pack_depth(fc, m), pack_depth(kc, m)], axis=0),
-            jnp.concatenate([pack_depth(ea, m), pack_depth([first, None, None, last], m)], axis=0),
-            jnp.concatenate([pack_depth(reach, m), pack_depth(reach, m)], axis=0))
+            pack_edges(jnp.concatenate([pack_depth(ea, m), pack_depth([first, None, None, last], m)], axis=0), m),
+            pack_depth(reach, m))
 
 
 def pair_unpack(axial, got, fa, fc, base, pa, pc, get, m):
-    across, depth = partners(axial, [g[0:1] for g in got], m)
+    across, depth = partners(axial, [g[0:1] for g in got[:4]], m)
     x = [base[i] + pc[i] * depth[i] for i in range(4)]
     for i in across:
         x[i] = x[i] + pa[i] * across[i]
-    ga = edges([g[0:1] for g in got], m)
-    second = [g[1:2] for g in got]
-    face = jnp.where(m.slot_low, second[3], second[2]) * m.zmask + edges(second, m)
+    ga = edges(got, m, 0)
+    second = [g[1:2] for g in got[:4]]
+    face = jnp.where(m.slot_low, second[3], second[2]) * m.zmask + edges(got, m, 1)
     face = face + jnp.where(m.slot_low, got[9][0:1], got[8][0:1]) * m.far
     depth = [spread(face, i, m) + NEAR * m.zhas * (pc[i] * fc[i]) for i in range(4)]
     across = {0: jnp.where(m.out0, second[0] + NEAR * (pa[0] * fa[0]), 0.0) + spread(ga, 0, m),
@@ -447,8 +446,9 @@
             slot = OFFSETS.index((-dx, -dz))
             source = send_x[r] if dz == 0 else send_z[r]
             target = got_refs[r].at[slot]
-            if edge is not None and abs(dx) + abs(dz) == 2:
-                source = send_far.at[r % 2, 0 if dx else 1]
+            if edge is not None:
+                target = got_refs[r].at[pl.ds(2 * slot, 2) if slot < 4 else pl.ds(4 + slot, 1)]
+                source = source if slot < 4 else send_far.at[r % 2, 0 if dx else 1]
             if r == 0:
                 target = got_refs[0].at[pl.ds(3 * slot, 3) if slot < 4 else pl.ds(8 + slot, 1)]
                 source = source if slot < 4 else send_edge
@@ -460,6 +460,8 @@
         pltpu.make_async_copy(got_refs[r], got_refs[r], round_sem.at[1, r]).wait()
         if r == 0:
             return [got_refs[0][3 * k:3 * k + 3] if k < 4 else got_refs[0][8 + k:9 + k] for k in range(8)]
+        if ROUNDS[r][1] == 10:
+            return [got_refs[r][2 * k:2 * k + 2] if k < 4 else got_refs[r][4 + k:5 + k] for k in range(10)]
         return [got_refs[r][k] for k in range(ROUNDS[r][1])]
 
     def send_faces(r, along_axis, along_depth):
@@ -630,9 +632,10 @@
         pltpu.VMEM((4, 4, 8, 128), f32), pltpu.VMEM((4, 32, 128), f32), pltpu.SemaphoreType.DMA((2, 5)),
     ]
     scratch += [pltpu.VMEM((n, 8, 128), f32) for n, _ in ROUNDS] * 2
-    scratch += [pltpu.VMEM((k, n, 8, 128) if r else (16, 8, 128), f32) for r, (n, k) in enumerate(ROUNDS)]
+    packed = {0: (16, 8, 128), 4: (14, 8, 128), 5: (14, 8, 128)}
+    scratch += [pltpu.VMEM(packed.get(r, (k, n, 8, 128)), f32) for r, (n, k) in enumerate(ROUNDS)]
     scratch += [
-        pltpu.VMEM((1, 8, 128), f32), pltpu.VMEM((2, 2, 2, 8, 128), f32), pltpu.SemaphoreType.DMA((2, len(ROUNDS))),
+        pltpu.VMEM((1, 8, 128), f32), pltpu.VMEM((2, 2, 1, 8, 128), f32), pltpu.SemaphoreType.DMA((2, len(ROUNDS))),
         pltpu.VMEM((2, 1, 128), f32), pltpu.VMEM((MEMBERS[0] - 1, 1, 128), f32), pltpu.VMEM((MEMBERS[1] - 1, 1, 128), f32),
         pltpu.SemaphoreType.DMA((2, 2)),
         pltpu.VMEM((9, 32, 128), f32), pltpu.VMEM((9, 32, 128), f32), pltpu.SemaphoreType.DMA((5, 4)),

time: 52.7 us -> 52.5 us (level)
  no operation moved by 1% of the time
where the time goes in v7:
time: 52.5 us; the launch traced here: 52.4 us
  Pallas kernels  51.8 us (99%)
  between operations  0.64 us (1%)
    pallas_call x1, Pallas kernels, body(): pl.pallas_call(kernel, out_shape=[pltpu.VMEM((9, 32, 128), f32), pltpu.VM...  51 us

profile of v7, /device:TPU:1, one launch (start us, length us, event | category | flops | bytes accessed | tf_op | source)
XLA Modules:
  0.0 52.4 jit_solution(16941405679421167656)
XLA Ops:
  0.6 51.0 %duct_step.1 = (f32[9,32,128]{2,1,0:T(8,128)S(1)}, f32[1,128]{1,0:T(1,128)S(1)}) custom-call(f32[6,4,512]{2,1,0:T(4,128)} %bitcast.11, f32[2,4,512]{2,1,0:T(4,128)} %bitcast.12, f32[136,8,128]{2,1,0:T(8,128)} %constant.2.clone.table_hbm), custom_call_target="tpu_custom_call" | custom-call | tf_op jit(solution)/shard_map/duct_step/pallas_call | solution.py:643
  51.6 0.8 %combine.1 = (f32[6,4,512]{2,1,0:T(4,128)}, f32[2,4,512]{2,1,0:T(4,128)}, f32[2,4,512]{2,1,0:T(4,128)}) custom-call(f32[9,32,128]{2,1,0:T(8,128)S(1)} %get-tuple-element.8.home, f32[1,128]{1,0:T(1,128)S(1)} %get-tuple-element.9.total_ref), custom_call_target="tpu_custom_call" | custom-call | tf_op jit(solution)/shard_map/combine/pallas_call | solution.py:652
